TPU v7x, 128 devices: a whole 4x4x4 slice. The times are simulated.
128 devices in a mesh: col: 8 (over z, core), hgt: 16 (over x, y).
Axes of the slice: x: 4, y: 4, z: 4, core: 2. Of those that a mesh axis runs over, the one named last changes fastest.
Arguments:
- efield_lattice_vector: float32 [3, 128, 384, 1024], P(None, 'col', 'hgt'), may hold values from -6 to 6
- hfield_lattice_vector: float32 [3, 128, 384, 1024], P(None, 'col', 'hgt'), may hold values from -6 to 6
- cell_temp: float32 [128, 384, 1024], P('col', 'hgt'), may hold values from -3 to 1
- region_tags: int32 [128, 384, 1024], P('col', 'hgt'), may hold values from 0 to 2
- block_owner: int32 [8, 16, 16, 24, 8, 1], P('col', 'hgt'), may hold values from 0 to 127; in each aligned block of 3072 rows (0 to 3071, 3072 to 6143, ..., all dimensions but the last counted through in order) at most 48 rows name the same one
- block_node: int32 [8, 16, 16, 24, 8], P('col', 'hgt'), may hold values from 0 to 383
- node_enthalpy: float32 [49152, 128], P(('col', 'hgt')), may hold values from -1.5 to 2.5
Outputs:
- e_out: float32 [3, 128, 384, 1024], P(None, 'col', 'hgt')
- h_out: float32 [3, 128, 384, 1024], P(None, 'col', 'hgt')
- node_temp: float32 [49152, 128], P(('col', 'hgt'))
Inputs may be any that keep to these rules, and one draw needn't show every extreme that they name: `block_owner`: among the margin blocks of one device, no partition is named by more than 48 blocks, a bound that the blocks of some device reach.
All inputs are finite; a program needn't handle non-finite values.
Results may differ from a plain program's by a relative error of at most 0.0003.
Values sent between devices are 32-bit elements; how exact they have to be, the bound alone decides.
A program may use at most 320 MiB of HBM per device.

v0:
```python
import jax
import jax.numpy as jnp
from jax import lax
from jax.sharding import PartitionSpec as P

PTS = 128
STEPS = 4


def from_behind(block, axis, distance):
    devices = range(lax.axis_size(axis))
    route = [(i - distance, i) for i in devices if i - distance in devices]
    return lax.ppermute(block, axis, route)


def coefficients(cell_temp, region_tags):
    frac = jax.nn.sigmoid(2.0 * cell_temp)
    lean = region_tags == 0
    fat = region_tags == 1
    eps_frozen = jnp.where(lean, 4.0, jnp.where(fat, 2.5, 5.0))
    eps_thawed = jnp.where(lean, 50.0, jnp.where(fat, 6.0, 10.0))
    sig_frozen = jnp.where(lean, 0.2, jnp.where(fat, 0.05, 0.1))
    melted_conductance = jnp.where(lean, 8.0, jnp.where(fat, 0.4, 1.0))
    eps = eps_frozen + (eps_thawed - eps_frozen) * frac
    sigma = sig_frozen + (melted_conductance - sig_frozen) * frac
    loss = sigma * 0.55 / (2.0 * eps)
    ca = (1.0 - loss) / (1.0 + loss)
    cb = 0.55 / (eps * (1.0 + loss))
    return (sigma, ca, cb)


def forward(field, plane, axis):
    size = field.shape[axis]
    return jnp.concatenate([lax.slice_in_dim(field, 1, size, axis=axis), plane], axis) - field


def backward(field, plane, axis):
    size = field.shape[axis]
    return field - jnp.concatenate([plane, lax.slice_in_dim(field, 0, size - 1, axis=axis)], axis)


def curl(diff, comps, planes_x, planes_z, plane_y):
    fx, fy, fz = comps
    dx_y = diff(fy, planes_x[0], 0)
    dx_z = diff(fz, planes_x[1], 0)
    dz_x = diff(fx, planes_z[0], 1)
    dz_y = diff(fy, planes_z[1], 1)
    dy_x = diff(fx, plane_y, 2)
    dy_z = diff(fz, plane_y, 2)
    return jnp.stack([dy_z - dz_y, dz_x - dx_z, dx_y - dy_x])


def tissue_warmth_kelvin(heat_content_per_mass):
    return jnp.where(
        heat_content_per_mass < 0.0,
        heat_content_per_mass / 2.0,
        jnp.where(heat_content_per_mass > 1.0, (heat_content_per_mass - 1.0) / 3.0, 0.0),
    )


def per_device(
    efield_lattice_vector,
    hfield_lattice_vector,
    cell_temp,
    region_tags,
    block_owner,
    block_node,
    node_enthalpy,
):
    size_x, size_z, size_y = cell_temp.shape
    n_col = lax.axis_size("col")
    n_hgt = lax.axis_size("hgt")
    sigma, ca, cb = coefficients(cell_temp, region_tags)
    empty_height_plane = jnp.zeros((size_x, size_z, 1), jnp.float32)
    power = jnp.zeros(cell_temp.shape, jnp.float32)
    for step in range(STEPS):
        next_x = from_behind(efield_lattice_vector[1:3, :1], "col", -1)
        next_z = from_behind(efield_lattice_vector[0:2, :, :1], "hgt", -1)
        hfield_lattice_vector = hfield_lattice_vector - 0.55 * curl(
            forward,
            (efield_lattice_vector[0], efield_lattice_vector[1], efield_lattice_vector[2]),
            next_x,
            next_z,
            empty_height_plane,
        )
        prev_x = from_behind(hfield_lattice_vector[1:3, size_x - 1 :], "col", 1)
        previous_depth = from_behind(hfield_lattice_vector[0:2, :, size_z - 1 :], "hgt", 1)
        efield_lattice_vector = ca * efield_lattice_vector + cb * curl(
            backward,
            (hfield_lattice_vector[0], hfield_lattice_vector[1], hfield_lattice_vector[2]),
            prev_x,
            previous_depth,
            empty_height_plane,
        )
        power = power + sigma * (
            efield_lattice_vector[0] * efield_lattice_vector[0]
            + efield_lattice_vector[1] * efield_lattice_vector[1]
            + efield_lattice_vector[2] * efield_lattice_vector[2]
        )
    absorbed = power / STEPS
    blocks = absorbed.reshape(-1, PTS)
    count_blocks = blocks.shape[0]
    n_dev = n_col * n_hgt
    capacity = 2 * count_blocks // n_dev
    owners = block_owner.reshape(-1)
    nodes = block_node.reshape(-1).astype(jnp.float32)
    onehot = (owners[:, None] == jnp.arange(n_dev, dtype=jnp.int32)[None, :]).astype(jnp.int32)
    ranks = jnp.sum((jnp.cumsum(onehot, axis=0) - 1) * onehot, axis=1)
    where_to = owners * capacity + ranks
    send_vals = jnp.zeros((n_dev * capacity, PTS), jnp.float32).at[where_to].set(blocks)
    send_nodes = jnp.full((n_dev * capacity,), -1.0, jnp.float32).at[where_to].set(nodes)
    recv_vals, recv_nodes = (
        lax.all_to_all(send_vals, ("col", "hgt"), split_axis=0, concat_axis=0, tiled=True),
        lax.all_to_all(send_nodes, ("col", "hgt"), split_axis=0, concat_axis=0, tiled=True),
    )
    node_count = node_enthalpy.shape[0]
    choose_entries = (
        recv_nodes[:, None] == jnp.arange(node_count, dtype=jnp.float32)[None, :]
    ).astype(jnp.float32)
    heat = lax.dot_general(
        choose_entries,
        recv_vals,
        (((0,), (0,)), ((), ())),
        precision=lax.Precision.HIGHEST,
        preferred_element_type=jnp.float32,
    )
    heat_content_per_mass = node_enthalpy + 0.25 * heat
    return (
        efield_lattice_vector,
        hfield_lattice_vector,
        tissue_warmth_kelvin(heat_content_per_mass),
    )


def solution(mesh):
    placed = (
        P(None, "col", "hgt", None),
        P(None, "col", "hgt", None),
        P("col", "hgt", None),
        P("col", "hgt", None),
        P("col", "hgt", None, None, None, None),
        P("col", "hgt", None, None, None),
        P(("col", "hgt"), None),
    )
    return jax.shard_map(
        per_device,
        mesh=mesh,
        in_specs=placed,
        out_specs=(
            P(None, "col", "hgt", None),
            P(None, "col", "hgt", None),
            P(("col", "hgt"), None),
        ),
        check_vma=False,
    )
```

profile of v0, /device:TPU:1, one launch (start us, length us, event | category | flops | bytes accessed | tf_op | source)
XLA Modules:
  0.0 299.0 jit_solution(9053164375514874012)
XLA Ops:
  4.2 3.3 %collective-permute-start.1 = (f32[2,1,24,1024]{3,2,1,0:T(8,128)S(1)}, f32[2,1,24,1024]{3,2,1,0:T(8,128)S(1)}, u32[]{:S(2)}, u32[]{:S(2)}) collective-permute-start(f32[2,1,24,1024]{3,2,1,0:T(8,128)S(1)} %slice.454), channel_id=1, source_target_pairs={{16,0},{32,16},{48,32},{64,48},{80,64},{96,80},{112,96},{17,1},{33... | collective-permute-start | bytes 589832 | tf_op jit(solution)/shard_map/ppermute | solution.py:13
  13.7 11.8 %scatter_custom_fusion = f32[6144]{0:T(1024)S(1)} fusion(s32[3072]{0:T(1024)S(1)} %bitcast.293, f32[3072]{0:T(1024)S(1)} %reshape.150, f32[]{:T(128)} %constant.15.clone.1), kind=kCustom, calls=%fused_computation.182 | custom fusion | bytes 24580 | tf_op jit(solution)/shard_map/scatter | solution.py:111
  26.2 12.2 %all-to-all-start = ((f32[128,48,1]{1,2,0:T(1,128)}), f32[128,48,1]{1,2,0:T(1,128)}, u32[]{:S(2)}, u32[]{:S(2)}) async-start(f32[128,48,1]{1,2,0:T(1,128)} %bitcast.77), calls=%async_computation | async-start | bytes 131072 | tf_op jit(solution)/shard_map/all_to_all | solution.py:114
  40.8 2.9 subtract_divide_fusion
  54.5 3.7 %collective-permute-start.3 = (f32[2,1,24,1024]{3,2,1,0:T(8,128)S(1)}, f32[2,1,24,1024]{3,2,1,0:T(8,128)S(1)}, u32[]{:S(2)}, u32[]{:S(2)}) collective-permute-start(f32[2,1,24,1024]{3,2,1,0:T(8,128)S(1)} %slice.594), channel_id=1, source_target_pairs={{0,16},{16,32},{32,48},{48,64},{64,80},{80,96},{96,112},{1,17},{17... | collective-permute-start | bytes 589832 | tf_op jit(solution)/shard_map/ppermute | solution.py:13
  58.3 3.4 %collective-permute-start.2 = (f32[2,16,1,1024]{3,2,1,0:T(1,128)S(1)}, f32[2,16,1,1024]{3,2,1,0:T(1,128)S(1)}, u32[]{:S(2)}, u32[]{:S(2)}) collective-permute-start(f32[2,16,1,1024]{3,2,1,0:T(1,128)S(1)} %slice.588), channel_id=1, source_target_pairs={{0,1},{1,2},{2,3},{3,4},{4,5},{5,6},{6,7},{7,8},{8,9},{9,10},{10,1... | collective-permute-start | bytes 393224 | tf_op jit(solution)/shard_map/ppermute | solution.py:13
  65.3 5.0 %fusion.22 = (f32[1,16,24,1024]{3,2,1,0:T(8,128)}, f32[1,16,24,1024]{3,2,1,0:T(8,128)}) fusion(f32[16,23,1024]{2,1,0:T(8,128)S(1)} %bitcast.284, f32[16,1,1024]{2,1,0:T(1,128)S(1)} %get-tuple-element.90, f32[16,24,1023]{2,1,0:T(8,128)S(1)} %bitcast.283, f32[3,16,24,1024]{3,2,1,0:T(8,128)S(1)} %fusion.1, f32[16,24,1023]{2,1,0:T(8,128)S(1)} %bitcast.279, ...), kind=kLoop, calls=%fused_computation.56 | loop fusion | flops 3145728 | bytes 14152704 | tf_op jit(solution)/shard_map/stack | solution.py:50
  70.3 3.5 %fusion.2 = f32[3,16,24,1024]{3,2,1,0:T(8,128)S(1)} fusion(f32[1,16,24,1024]{3,2,1,0:T(8,128)} %get-tuple-element.49, f32[1,16,24,1024]{3,2,1,0:T(8,128)S(1)} %get-tuple-element.51, f32[1,16,24,1024]{3,2,1,0:T(8,128)} %get-tuple-element.48, f32[3,16,24,1024]{3,2,1,0:T(8,128)S(1)} %bitcast.276, f32[16,24,1024]{2,1,0:T(8,128)} %multiply_divide_fusion, ...), kind=kLoop, calls=%fused_computation.7 | loop fusion | flops 5898240 | bytes 17301504 | tf_op jit(solution)/shard_map/add | solution.py:88
  81.7 2.8 collective-permute-done.5
  93.8 4.9 %collective-permute-start.6 = (f32[2,16,1,1024]{3,2,1,0:T(1,128)S(1)}, f32[2,16,1,1024]{3,2,1,0:T(1,128)S(1)}, u32[]{:S(2)}, u32[]{:S(2)}) collective-permute-start(f32[2,16,1,1024]{3,2,1,0:T(1,128)S(1)} %slice.618), channel_id=1, source_target_pairs={{0,1},{1,2},{2,3},{3,4},{4,5},{5,6},{6,7},{7,8},{8,9},{9,10},{10,1... | collective-permute-start | bytes 393224 | tf_op jit(solution)/shard_map/ppermute | solution.py:13
  102.9 4.4 %fusion.32 = (f32[1,16,24,1024]{3,2,1,0:T(8,128)}, f32[1,16,24,1024]{3,2,1,0:T(8,128)}) fusion(f32[16,23,1024]{2,1,0:T(8,128)S(1)} %bitcast.286, f32[16,1,1024]{2,1,0:T(1,128)S(1)} %get-tuple-element.86, f32[16,24,1023]{2,1,0:T(8,128)S(1)} %bitcast.285, f32[3,16,24,1024]{3,2,1,0:T(8,128)S(1)} %fusion.3, f32[16,24,1023]{2,1,0:T(8,128)S(1)} %bitcast.280, ...), kind=kLoop, calls=%fused_computation.74 | loop fusion | flops 3145728 | bytes 14152704 | tf_op jit(solution)/shard_map/stack | solution.py:50
  107.3 5.6 %fusion.4 = f32[3,16,24,1024]{3,2,1,0:T(8,128)S(1)} fusion(f32[1,16,24,1024]{3,2,1,0:T(8,128)} %get-tuple-element.35, f32[1,16,24,1024]{3,2,1,0:T(8,128)} %get-tuple-element.37, f32[1,16,24,1024]{3,2,1,0:T(8,128)} %get-tuple-element.34, f32[16,24,1024]{2,1,0:T(8,128)} %multiply_divide_fusion, f32[16,24,1024]{2,1,0:T(8,128)} %get-tuple-element.3, ...), kind=kLoop, calls=%fused_computation.11 | loop fusion | flops 11796480 | bytes 22020096 | tf_op jit(solution)/shard_map/add | solution.py:88
  116.7 3.3 %collective-permute-start.9 = (f32[2,1,24,1024]{3,2,1,0:T(8,128)S(1)}, f32[2,1,24,1024]{3,2,1,0:T(8,128)S(1)}, u32[]{:S(2)}, u32[]{:S(2)}) collective-permute-start(f32[2,1,24,1024]{3,2,1,0:T(8,128)S(1)} %slice.640), channel_id=1, source_target_pairs={{16,0},{32,16},{48,32},{64,48},{80,64},{96,80},{112,96},{17,1},{33... | collective-permute-start | bytes 589832 | tf_op jit(solution)/shard_map/ppermute | solution.py:13
  120.0 4.6 %collective-permute-done.9 = f32[2,1,24,1024]{3,2,1,0:T(8,128)S(1)} collective-permute-done((f32[2,1,24,1024]{3,2,1,0:T(8,128)S(1)}, f32[2,1,24,1024]{3,2,1,0:T(8,128)S(1)}, u32[]{:S(2)}, u32[]{:S(2)}) %collective-permute-start.9) | collective-permute-done | bytes 196640 | tf_op jit(solution)/shard_map/ppermute | solution.py:13
  127.4 4.6 %fusion.37 = (f32[1,16,24,1024]{3,2,1,0:T(8,128)}, f32[1,16,24,1024]{3,2,1,0:T(8,128)}) fusion(f32[16,1,1024]{2,1,0:T(1,128)S(1)} %get-tuple-element.84, f32[16,23,1024]{2,1,0:T(8,128)S(1)} %slice.633, f32[16,24,1023]{2,1,0:T(8,128)S(1)} %slice.631, f32[3,16,24,1024]{3,2,1,0:T(8,128)S(1)} %fusion.4, f32[16,24,1023]{2,1,0:T(8,128)S(1)} %slice.644, ...), kind=kLoop, calls=%fused_computation.83 | loop fusion | flops 3145728 | bytes 14152704 | tf_op jit(solution)/shard_map/stack | solution.py:50
  132.0 4.9 %fusion.5 = f32[3,16,24,1024]{3,2,1,0:T(8,128)S(1)} fusion(f32[1,16,24,1024]{3,2,1,0:T(8,128)} %get-tuple-element.28, f32[1,16,24,1024]{3,2,1,0:T(8,128)} %get-tuple-element.30, f32[1,16,24,1024]{3,2,1,0:T(8,128)} %get-tuple-element.27, f32[1,16,24,1024]{3,2,1,0:T(8,128)} %copy-done.14, f32[1,16,24,1024]{3,2,1,0:T(8,128)} %copy-done.12, ...), kind=kLoop, calls=%fused_computation.13 | loop fusion | flops 14155776 | bytes 23592960 | tf_op jit(solution)/shard_map/sub | solution.py:79
  139.3 4.9 %collective-permute-start.10 = (f32[2,16,1,1024]{3,2,1,0:T(1,128)S(1)}, f32[2,16,1,1024]{3,2,1,0:T(1,128)S(1)}, u32[]{:S(2)}, u32[]{:S(2)}) collective-permute-start(f32[2,16,1,1024]{3,2,1,0:T(1,128)S(1)} %slice.648), channel_id=1, source_target_pairs={{0,1},{1,2},{2,3},{3,4},{4,5},{5,6},{6,7},{7,8},{8,9},{9,10},{10,1... | collective-permute-start | bytes 393224 | tf_op jit(solution)/shard_map/ppermute | solution.py:13
  146.5 3.1 %slice_bitcast_fusion.21 = (f32[16,24,1024]{2,1,0:T(8,128)}, f32[1,16,24,1024]{3,2,1,0:T(8,128)}, f32[16,24,1024]{2,1,0:T(8,128)}) fusion(f32[3,16,24,1024]{3,2,1,0:T(8,128)S(1)} %fusion.5, f32[1,15,24,1024]{3,2,1,0:T(8,128)S(1)} %get-tuple-element.25, f32[1,1,24,1024]{3,2,1,0:T(8,128)S(1)} %get-tuple-element.66, ...), kind=kLoop, calls=%fused_computation.138 | loop fusion | flops 1966080 | bytes 12582912 | tf_op jit(solution)/shard_map/squeeze | solution.py:90
  149.6 5.8 %fusion.42 = (f32[1,16,24,1024]{3,2,1,0:T(8,128)}, f32[1,16,24,1024]{3,2,1,0:T(8,128)}) fusion(f32[16,23,1024]{2,1,0:T(8,128)} %bitcast.288, f32[16,1,1024]{2,1,0:T(1,128)S(1)} %get-tuple-element.82, f32[16,24,1023]{2,1,0:T(8,128)} %bitcast.287, f32[3,16,24,1024]{3,2,1,0:T(8,128)S(1)} %fusion.5, f32[16,24,1023]{2,1,0:T(8,128)} %bitcast.281, ...), kind=kLoop, calls=%fused_computation.92 | loop fusion | flops 3145728 | bytes 14152704 | tf_op jit(solution)/shard_map/stack | solution.py:50
  155.5 6.2 %fusion.6 = f32[3,16,24,1024]{3,2,1,0:T(8,128)S(1)} fusion(f32[1,16,24,1024]{3,2,1,0:T(8,128)} %get-tuple-element.21, f32[1,16,24,1024]{3,2,1,0:T(8,128)} %get-tuple-element.23, f32[1,16,24,1024]{3,2,1,0:T(8,128)} %get-tuple-element.20, f32[16,24,1024]{2,1,0:T(8,128)} %multiply_divide_fusion, f32[16,24,1024]{2,1,0:T(8,128)} %get-tuple-element.3, ...), kind=kLoop, calls=%fused_computation.15 | loop fusion | flops 17694720 | bytes 26738688 | tf_op jit(solution)/shard_map/add | solution.py:88
  165.4 3.3 %collective-permute-start.13 = (f32[2,1,24,1024]{3,2,1,0:T(8,128)S(1)}, f32[2,1,24,1024]{3,2,1,0:T(8,128)S(1)}, u32[]{:S(2)}, u32[]{:S(2)}) collective-permute-start(f32[2,1,24,1024]{3,2,1,0:T(8,128)S(1)} %slice.670), channel_id=1, source_target_pairs={{16,0},{32,16},{48,32},{64,48},{80,64},{96,80},{112,96},{17,1},{33... | collective-permute-start | bytes 589832 | tf_op jit(solution)/shard_map/ppermute | solution.py:13
  168.7 4.6 %collective-permute-done.13 = f32[2,1,24,1024]{3,2,1,0:T(8,128)S(1)} collective-permute-done((f32[2,1,24,1024]{3,2,1,0:T(8,128)S(1)}, f32[2,1,24,1024]{3,2,1,0:T(8,128)S(1)}, u32[]{:S(2)}, u32[]{:S(2)}) %collective-permute-start.13) | collective-permute-done | bytes 196640 | tf_op jit(solution)/shard_map/ppermute | solution.py:13
  176.1 4.5 %fusion.47 = (f32[1,16,24,1024]{3,2,1,0:T(8,128)}, f32[1,16,24,1024]{3,2,1,0:T(8,128)}) fusion(f32[16,1,1024]{2,1,0:T(1,128)S(1)} %get-tuple-element.80, f32[16,23,1024]{2,1,0:T(8,128)S(1)} %slice.663, f32[16,24,1023]{2,1,0:T(8,128)S(1)} %slice.661, f32[3,16,24,1024]{3,2,1,0:T(8,128)S(1)} %fusion.6, f32[16,24,1023]{2,1,0:T(8,128)S(1)} %slice.674, ...), kind=kLoop, calls=%fused_computation.101 | loop fusion | flops 3145728 | bytes 14152704 | tf_op jit(solution)/shard_map/stack | solution.py:50
  180.7 8.0 %fusion.7 = f32[3,16,24,1024]{3,2,1,0:T(8,128)S(1)} fusion(f32[1,16,24,1024]{3,2,1,0:T(8,128)} %get-tuple-element.14, f32[1,16,24,1024]{3,2,1,0:T(8,128)} %get-tuple-element.16, f32[1,16,24,1024]{3,2,1,0:T(8,128)} %get-tuple-element.13, f32[1,16,24,1024]{3,2,1,0:T(8,128)} %get-tuple-element.28, f32[1,16,24,1024]{3,2,1,0:T(8,128)} %get-tuple-element.30, ...), kind=kLoop, calls=%fused_computation.17 | loop fusion | flops 18874368 | bytes 28311552 | tf_op jit(solution)/shard_map/sub | solution.py:79
  191.1 5.0 %collective-permute-start.14 = (f32[2,16,1,1024]{3,2,1,0:T(1,128)S(1)}, f32[2,16,1,1024]{3,2,1,0:T(1,128)S(1)}, u32[]{:S(2)}, u32[]{:S(2)}) collective-permute-start(f32[2,16,1,1024]{3,2,1,0:T(1,128)S(1)} %slice.678), channel_id=1, source_target_pairs={{0,1},{1,2},{2,3},{3,4},{4,5},{5,6},{6,7},{7,8},{8,9},{9,10},{10,1... | collective-permute-start | bytes 393224 | tf_op jit(solution)/shard_map/ppermute | solution.py:13
  198.2 2.9 slice_bitcast_fusion.17
  201.1 5.8 %fusion.52 = (f32[1,16,24,1024]{3,2,1,0:T(8,128)}, f32[1,16,24,1024]{3,2,1,0:T(8,128)}) fusion(f32[16,23,1024]{2,1,0:T(8,128)} %bitcast.290, f32[16,1,1024]{2,1,0:T(1,128)S(1)} %get-tuple-element.78, f32[16,24,1023]{2,1,0:T(8,128)} %bitcast.289, f32[3,16,24,1024]{3,2,1,0:T(8,128)S(1)} %fusion.7, f32[16,24,1023]{2,1,0:T(8,128)} %bitcast.282, ...), kind=kLoop, calls=%fused_computation.110 | loop fusion | flops 3145728 | bytes 14152704 | tf_op jit(solution)/shard_map/stack | solution.py:50
  206.9 8.9 %fusion.8 = f32[3,16,24,1024]{3,2,1,0:T(8,128)S(1)} fusion(f32[1,16,24,1024]{3,2,1,0:T(8,128)} %get-tuple-element.7, f32[1,16,24,1024]{3,2,1,0:T(8,128)} %get-tuple-element.9, f32[1,16,24,1024]{3,2,1,0:T(8,128)} %get-tuple-element.6, f32[16,24,1024]{2,1,0:T(8,128)} %multiply_divide_fusion, f32[16,24,1024]{2,1,0:T(8,128)} %get-tuple-element.3, ...), kind=kLoop, calls=%fused_computation.19 | loop fusion | flops 23592960 | bytes 31457280 | tf_op jit(solution)/shard_map/add | solution.py:88
  222.0 10.2 %scatter_custom_fusion.1 = f32[6144,128]{1,0:T(8,128)} fusion(s32[3072]{0:T(1024)} %bitcast.294, f32[3072,128]{1,0:T(8,128)} %reshape.158, f32[]{:T(128)} %constant.14.clone.1), kind=kCustom, calls=%fused_computation.119 | custom fusion | bytes 3146240 | tf_op jit(solution)/shard_map/scatter | solution.py:110
  232.3 16.5 %all-to-all-start.1 = ((f32[128,48,128]{2,1,0:T(8,128)}), f32[128,48,128]{2,1,0:T(8,128)S(1)}, u32[]{:S(2)}, u32[]{:S(2)}) async-start(f32[128,48,128]{2,1,0:T(8,128)} %bitcast.79), calls=%async_computation.1 | async-start | bytes 6291456 | tf_op jit(solution)/shard_map/all_to_all | solution.py:113
  251.0 38.7 %all-to-all-done.1 = f32[128,48,128]{2,1,0:T(8,128)S(1)} async-done(((f32[128,48,128]{2,1,0:T(8,128)}), f32[128,48,128]{2,1,0:T(8,128)S(1)}, u32[]{:S(2)}, u32[]{:S(2)}) %all-to-all-start.1) | async-done | bytes 3145760 | tf_op jit(solution)/shard_map/all_to_all | solution.py:113
  289.7 9.0 %select_select_fusion = f32[384,128]{1,0:T(8,128)} fusion(f32[384,128]{1,0:T(8,128)S(1)} %copy-done.27, f32[6144,128]{1,0:T(8,128)S(1)} %bitcast.291, f32[6144]{0:T(1024)S(1)} %eq.64), kind=kOutput, calls=%fused_computation.162 | convolution fusion | flops 3626680320 | bytes 3563520 | tf_op jit(solution)/shard_map/dot_general | solution.py:120
  (191 shorter events, 78.8 us)
Async XLA Ops:
  1.9 46.2 %collective-permute-start = (f32[2,16,1,1024]{3,2,1,0:T(1,128)S(1)}, f32[2,16,1,1024]{3,2,1,0:T(1,128)S(1)}, u32[]{:S(2)}, u32[]{:S(2)}) collective-permute-start(f32[2,16,1,1024]{3,2,1,0:T(1,128)S(1)} %slice.448), channel_id=1, source_target_pairs={{1,0},{2,1},{3,2},{4,3},{5,4},{6,5},{7,6},{8,7},{9,8},{10,9},{11,1... | collective-permute-start | bytes 393224 | tf_op jit(solution)/shard_map/ppermute | solution.py:13
  4.2 44.0 %collective-permute-start.1 = (f32[2,1,24,1024]{3,2,1,0:T(8,128)S(1)}, f32[2,1,24,1024]{3,2,1,0:T(8,128)S(1)}, u32[]{:S(2)}, u32[]{:S(2)}) collective-permute-start(f32[2,1,24,1024]{3,2,1,0:T(8,128)S(1)} %slice.454), channel_id=1, source_target_pairs={{16,0},{32,16},{48,32},{64,48},{80,64},{96,80},{112,96},{17,1},{33... | collective-permute-start | bytes 589832 | tf_op jit(solution)/shard_map/ppermute | solution.py:13
  13.7 26.4 %copy-start.26 = (s32[3072,1]{0,1:T(1,128)}, s32[3072,1]{0,1:T(1,128)S(1)}, u32[]{:S(2)}) copy-start(s32[3072,1]{0,1:T(1,128)S(1)} %compare_select_fusion) | copy-start | bytes 36868
  26.2 206.1 %all-to-all-start = ((f32[128,48,1]{1,2,0:T(1,128)}), f32[128,48,1]{1,2,0:T(1,128)}, u32[]{:S(2)}, u32[]{:S(2)}) async-start(f32[128,48,1]{1,2,0:T(1,128)} %bitcast.77), calls=%async_computation | async-start | bytes 131072 | tf_op jit(solution)/shard_map/all_to_all | solution.py:114
  40.1 7.3 %slice-start = ((s8[4718592]{0:T(1024)(128)(4,1)}), s8[4194304]{0:T(1024)(128)(4,1)S(1)}, s32[]{:S(2)}) async-start(s8[4718592]{0:T(1024)(128)(4,1)} %bitcast.275), calls=%async_computation.2 | async-start | bytes 8388608
  40.8 6.6 %slice-start.1 = ((s8[4718592]{0:T(1024)(128)(4,1)}), s8[524288]{0:T(1024)(128)(4,1)S(1)}, s32[]{:S(2)}) async-start(s8[4718592]{0:T(1024)(128)(4,1)} %bitcast.275), calls=%async_computation.3 | async-start | bytes 1048576
  51.6 37.5 %copy-start.1 = (f32[1,16,24,1024]{3,2,1,0:T(8,128)}, f32[1,16,24,1024]{3,2,1,0:T(8,128)S(1)}, u32[]{:S(2)}) copy-start(f32[1,16,24,1024]{3,2,1,0:T(8,128)S(1)} %get-tuple-element.55) | copy-start | bytes 4718596
  51.6 37.5 %copy-start.4 = (f32[1,16,24,1024]{3,2,1,0:T(8,128)}, f32[1,16,24,1024]{3,2,1,0:T(8,128)S(1)}, u32[]{:S(2)}) copy-start(f32[1,16,24,1024]{3,2,1,0:T(8,128)S(1)} %get-tuple-element.56) | copy-start | bytes 4718596
  54.5 9.6 %collective-permute-start.3 = (f32[2,1,24,1024]{3,2,1,0:T(8,128)S(1)}, f32[2,1,24,1024]{3,2,1,0:T(8,128)S(1)}, u32[]{:S(2)}, u32[]{:S(2)}) collective-permute-start(f32[2,1,24,1024]{3,2,1,0:T(8,128)S(1)} %slice.594), channel_id=1, source_target_pairs={{0,16},{16,32},{32,48},{48,64},{64,80},{80,96},{96,112},{1,17},{17... | collective-permute-start | bytes 589832 | tf_op jit(solution)/shard_map/ppermute | solution.py:13
  58.3 5.8 %collective-permute-start.2 = (f32[2,16,1,1024]{3,2,1,0:T(1,128)S(1)}, f32[2,16,1,1024]{3,2,1,0:T(1,128)S(1)}, u32[]{:S(2)}, u32[]{:S(2)}) collective-permute-start(f32[2,16,1,1024]{3,2,1,0:T(1,128)S(1)} %slice.588), channel_id=1, source_target_pairs={{0,1},{1,2},{2,3},{3,4},{4,5},{5,6},{6,7},{7,8},{8,9},{9,10},{10,1... | collective-permute-start | bytes 393224 | tf_op jit(solution)/shard_map/ppermute | solution.py:13
  74.1 7.6 %collective-permute-start.4 = (f32[2,16,1,1024]{3,2,1,0:T(1,128)S(1)}, f32[2,16,1,1024]{3,2,1,0:T(1,128)S(1)}, u32[]{:S(2)}, u32[]{:S(2)}) collective-permute-start(f32[2,16,1,1024]{3,2,1,0:T(1,128)S(1)} %slice.604), channel_id=1, source_target_pairs={{1,0},{2,1},{3,2},{4,3},{5,4},{6,5},{7,6},{8,7},{9,8},{10,9},{11,1... | collective-permute-start | bytes 393224 | tf_op jit(solution)/shard_map/ppermute | solution.py:13
  77.5 7.0 %collective-permute-start.5 = (f32[2,1,24,1024]{3,2,1,0:T(8,128)S(1)}, f32[2,1,24,1024]{3,2,1,0:T(8,128)S(1)}, u32[]{:S(2)}, u32[]{:S(2)}) collective-permute-start(f32[2,1,24,1024]{3,2,1,0:T(8,128)S(1)} %slice.610), channel_id=1, source_target_pairs={{16,0},{32,16},{48,32},{64,48},{80,64},{96,80},{112,96},{17,1},{33... | collective-permute-start | bytes 589832 | tf_op jit(solution)/shard_map/ppermute | solution.py:13
  91.8 8.8 %collective-permute-start.7 = (f32[2,1,24,1024]{3,2,1,0:T(8,128)S(1)}, f32[2,1,24,1024]{3,2,1,0:T(8,128)S(1)}, u32[]{:S(2)}, u32[]{:S(2)}) collective-permute-start(f32[2,1,24,1024]{3,2,1,0:T(8,128)S(1)} %slice.624), channel_id=1, source_target_pairs={{0,16},{16,32},{32,48},{48,64},{64,80},{80,96},{96,112},{1,17},{17... | collective-permute-start | bytes 589832 | tf_op jit(solution)/shard_map/ppermute | solution.py:13
  93.8 6.8 %collective-permute-start.6 = (f32[2,16,1,1024]{3,2,1,0:T(1,128)S(1)}, f32[2,16,1,1024]{3,2,1,0:T(1,128)S(1)}, u32[]{:S(2)}, u32[]{:S(2)}) collective-permute-start(f32[2,16,1,1024]{3,2,1,0:T(1,128)S(1)} %slice.618), channel_id=1, source_target_pairs={{0,1},{1,2},{2,3},{3,4},{4,5},{5,6},{6,7},{7,8},{8,9},{9,10},{10,1... | collective-permute-start | bytes 393224 | tf_op jit(solution)/shard_map/ppermute | solution.py:13
  113.2 6.8 %collective-permute-start.8 = (f32[2,16,1,1024]{3,2,1,0:T(1,128)S(1)}, f32[2,16,1,1024]{3,2,1,0:T(1,128)S(1)}, u32[]{:S(2)}, u32[]{:S(2)}) collective-permute-start(f32[2,16,1,1024]{3,2,1,0:T(1,128)S(1)} %slice.634), channel_id=1, source_target_pairs={{1,0},{2,1},{3,2},{4,3},{5,4},{6,5},{7,6},{8,7},{9,8},{10,9},{11,1... | collective-permute-start | bytes 393224 | tf_op jit(solution)/shard_map/ppermute | solution.py:13
  116.7 7.9 %collective-permute-start.9 = (f32[2,1,24,1024]{3,2,1,0:T(8,128)S(1)}, f32[2,1,24,1024]{3,2,1,0:T(8,128)S(1)}, u32[]{:S(2)}, u32[]{:S(2)}) collective-permute-start(f32[2,1,24,1024]{3,2,1,0:T(8,128)S(1)} %slice.640), channel_id=1, source_target_pairs={{16,0},{32,16},{48,32},{64,48},{80,64},{96,80},{112,96},{17,1},{33... | collective-permute-start | bytes 589832 | tf_op jit(solution)/shard_map/ppermute | solution.py:13
  137.2 9.2 %collective-permute-start.11 = (f32[2,1,24,1024]{3,2,1,0:T(8,128)S(1)}, f32[2,1,24,1024]{3,2,1,0:T(8,128)S(1)}, u32[]{:S(2)}, u32[]{:S(2)}) collective-permute-start(f32[2,1,24,1024]{3,2,1,0:T(8,128)S(1)} %slice.654), channel_id=1, source_target_pairs={{0,16},{16,32},{32,48},{48,64},{64,80},{80,96},{96,112},{1,17},{17... | collective-permute-start | bytes 589832 | tf_op jit(solution)/shard_map/ppermute | solution.py:13
  139.3 7.1 %collective-permute-start.10 = (f32[2,16,1,1024]{3,2,1,0:T(1,128)S(1)}, f32[2,16,1,1024]{3,2,1,0:T(1,128)S(1)}, u32[]{:S(2)}, u32[]{:S(2)}) collective-permute-start(f32[2,16,1,1024]{3,2,1,0:T(1,128)S(1)} %slice.648), channel_id=1, source_target_pairs={{0,1},{1,2},{2,3},{3,4},{4,5},{5,6},{6,7},{7,8},{8,9},{9,10},{10,1... | collective-permute-start | bytes 393224 | tf_op jit(solution)/shard_map/ppermute | solution.py:13
  149.6 5.9 %copy-start.8 = (f32[1,16,24,1024]{3,2,1,0:T(8,128)S(1)}, f32[1,16,24,1024]{3,2,1,0:T(8,128)}, u32[]{:S(2)}) copy-start(f32[1,16,24,1024]{3,2,1,0:T(8,128)} %copy-done.7) | copy-start | bytes 4718596
  149.6 5.9 %copy-start.10 = (f32[1,16,24,1024]{3,2,1,0:T(8,128)S(1)}, f32[1,16,24,1024]{3,2,1,0:T(8,128)}, u32[]{:S(2)}) copy-start(f32[1,16,24,1024]{3,2,1,0:T(8,128)} %get-tuple-element.48) | copy-start | bytes 4718596
  149.6 5.9 %copy-start.11 = (f32[1,16,24,1024]{3,2,1,0:T(8,128)S(1)}, f32[1,16,24,1024]{3,2,1,0:T(8,128)}, u32[]{:S(2)}) copy-start(f32[1,16,24,1024]{3,2,1,0:T(8,128)} %get-tuple-element.49) | copy-start | bytes 4718596
  161.9 6.7 %collective-permute-start.12 = (f32[2,16,1,1024]{3,2,1,0:T(1,128)S(1)}, f32[2,16,1,1024]{3,2,1,0:T(1,128)S(1)}, u32[]{:S(2)}, u32[]{:S(2)}) collective-permute-start(f32[2,16,1,1024]{3,2,1,0:T(1,128)S(1)} %slice.664), channel_id=1, source_target_pairs={{1,0},{2,1},{3,2},{4,3},{5,4},{6,5},{7,6},{8,7},{9,8},{10,9},{11,1... | collective-permute-start | bytes 393224 | tf_op jit(solution)/shard_map/ppermute | solution.py:13
  165.4 7.9 %collective-permute-start.13 = (f32[2,1,24,1024]{3,2,1,0:T(8,128)S(1)}, f32[2,1,24,1024]{3,2,1,0:T(8,128)S(1)}, u32[]{:S(2)}, u32[]{:S(2)}) collective-permute-start(f32[2,1,24,1024]{3,2,1,0:T(8,128)S(1)} %slice.670), channel_id=1, source_target_pairs={{16,0},{32,16},{48,32},{64,48},{80,64},{96,80},{112,96},{17,1},{33... | collective-permute-start | bytes 589832 | tf_op jit(solution)/shard_map/ppermute | solution.py:13
  188.7 12.4 %copy-start = (f32[3,16,24,1024]{3,2,1,0:T(8,128)}, f32[3,16,24,1024]{3,2,1,0:T(8,128)S(1)}, u32[]{:S(2)}) copy-start(f32[3,16,24,1024]{3,2,1,0:T(8,128)S(1)} %fusion.7) | copy-start | bytes 14155780
  188.9 9.2 %collective-permute-start.15 = (f32[2,1,24,1024]{3,2,1,0:T(8,128)S(1)}, f32[2,1,24,1024]{3,2,1,0:T(8,128)S(1)}, u32[]{:S(2)}, u32[]{:S(2)}) collective-permute-start(f32[2,1,24,1024]{3,2,1,0:T(8,128)S(1)} %slice.684), channel_id=1, source_target_pairs={{0,16},{16,32},{32,48},{48,64},{64,80},{80,96},{96,112},{1,17},{17... | collective-permute-start | bytes 589832 | tf_op jit(solution)/shard_map/ppermute | solution.py:13
  191.1 7.1 %collective-permute-start.14 = (f32[2,16,1,1024]{3,2,1,0:T(1,128)S(1)}, f32[2,16,1,1024]{3,2,1,0:T(1,128)S(1)}, u32[]{:S(2)}, u32[]{:S(2)}) collective-permute-start(f32[2,16,1,1024]{3,2,1,0:T(1,128)S(1)} %slice.678), channel_id=1, source_target_pairs={{0,1},{1,2},{2,3},{3,4},{4,5},{5,6},{6,7},{7,8},{8,9},{9,10},{10,1... | collective-permute-start | bytes 393224 | tf_op jit(solution)/shard_map/ppermute | solution.py:13
  201.1 5.8 %copy-start.9 = (f32[1,16,24,1024]{3,2,1,0:T(8,128)S(1)}, f32[1,16,24,1024]{3,2,1,0:T(8,128)}, u32[]{:S(2)}) copy-start(f32[1,16,24,1024]{3,2,1,0:T(8,128)} %copy-done.7) | copy-start | bytes 4718596
  206.8 11.1 %copy-start.19 = (f32[16,24,1024]{2,1,0:T(8,128)S(1)}, f32[16,24,1024]{2,1,0:T(8,128)}, u32[]{:S(2)}) copy-start(f32[16,24,1024]{2,1,0:T(8,128)} %param.9) | copy-start | bytes 4718596
  206.8 11.1 %copy-start.21 = (pred[16,24,1024]{2,1,0:T(8,128)(4,1)S(1)}, pred[16,24,1024]{2,1,0:T(8,128)(4,1)}, u32[]{:S(2)}) copy-start(pred[16,24,1024]{2,1,0:T(8,128)(4,1)} %copy-done.20) | copy-start | bytes 1179652
  206.8 11.1 %copy-start.23 = (pred[16,24,1024]{2,1,0:T(8,128)(4,1)S(1)}, pred[16,24,1024]{2,1,0:T(8,128)(4,1)}, u32[]{:S(2)}) copy-start(pred[16,24,1024]{2,1,0:T(8,128)(4,1)} %copy-done.22) | copy-start | bytes 1179652
  232.3 57.4 %copy-start.27 = (f32[384,128]{1,0:T(8,128)S(1)}, f32[384,128]{1,0:T(8,128)}, u32[]{:S(2)}) copy-start(f32[384,128]{1,0:T(8,128)} %param.13) | copy-start | bytes 589828
  232.3 57.4 %all-to-all-start.1 = ((f32[128,48,128]{2,1,0:T(8,128)}), f32[128,48,128]{2,1,0:T(8,128)S(1)}, u32[]{:S(2)}, u32[]{:S(2)}) async-start(f32[128,48,128]{2,1,0:T(8,128)} %bitcast.79), calls=%async_computation.1 | async-start | bytes 6291456 | tf_op jit(solution)/shard_map/all_to_all | solution.py:113
  (18 other events, 49.2 us)
where the time goes:
time: 304 us; the launch traced here: 299 us
  other arithmetic  104 us (34%)
  starting transfers between devices  73.1 us (24%)
  waiting for transfers between devices  56.2 us (18%)
  local copies, waits for them, and re-layouts  54.7 us (18%)
  matrix products  9.01 us (3%)
    ppermute x16, starting transfers between devices, from_behind(): return lax.ppermute(block, axis, route)  44.5 us
    all_to_all x1, waiting for transfers between devices, per_device(): lax.all_to_all(send_vals, ('col', 'hgt'), split_axis=0, concat_axis=0, ti...  38.7 us
    another operation x8, other arithmetic, curl(): return jnp.stack([dy_z - dz_y, dz_x - dx_z, dx_y - dy_x])  34.2 us
    add x4, other arithmetic, per_device(): ca * efield_lattice_vector  24.2 us
    ppermute x16, waiting for transfers between devices, from_behind(): return lax.ppermute(block, axis, route)  17.5 us
    all_to_all x1, starting transfers between devices, per_device(): lax.all_to_all(send_vals, ('col', 'hgt'), split_axis=0, concat_axis=0, ti...  16.5 us
    sub x4, other arithmetic, per_device(): hfield_lattice_vector - 0.55 * curl(forward, (efield_lattice_vector[0], e...  16.3 us
    all_to_all x1, starting transfers between devices, per_device(): lax.all_to_all(send_nodes, ('col', 'hgt'), split_axis=0, concat_axis=0, t...  12.2 us
  transfers between devices with their start and end apart: 18, of which 9 were waited for; matrix products, arithmetic and copies ran while one was open for 51% of the time, Pallas kernels for 0%

commit v1 on v0

v1 whole, which is shorter than its diff:
```python
import jax
import jax.numpy as jnp
from jax import lax
from jax.experimental import pallas as pl
from jax.experimental.pallas import tpu as pltpu
from jax.sharding import PartitionSpec as P

STEPS = 4
COURANT = 0.55
MESH = pl.DeviceIdType.MESH
F32 = jnp.float32
ANY = pl.BlockSpec(memory_space=pl.ANY)
HBM = pl.BlockSpec(memory_space=pltpu.HBM)
VMEM = pl.BlockSpec(memory_space=pltpu.VMEM)
SMEM = pl.BlockSpec(memory_space=pltpu.SMEM)


def shifted_up(f):
    axis = f.ndim - 1
    lane = lax.broadcasted_iota(jnp.int32, f.shape, axis)
    sub = lax.broadcasted_iota(jnp.int32, f.shape, axis - 1)
    r = pltpu.roll(f, 127, axis)
    u = pltpu.roll(r, 7, axis - 1)
    return jnp.where(lane < 127, r, jnp.where(sub < 7, u, 0.0))


def shifted_down(f):
    axis = f.ndim - 1
    lane = lax.broadcasted_iota(jnp.int32, f.shape, axis)
    sub = lax.broadcasted_iota(jnp.int32, f.shape, axis - 1)
    r = pltpu.roll(f, 1, axis)
    u = pltpu.roll(r, 1, axis - 1)
    return jnp.where(lane > 0, r, jnp.where(sub > 0, u, 0.0))


def coefficients(temp, tags):
    frac = 1.0 / (1.0 + jnp.exp(-2.0 * temp))
    lean = tags == 0
    fat = tags == 1
    eps_frozen = jnp.where(lean, 4.0, jnp.where(fat, 2.5, 5.0))
    eps_span = jnp.where(lean, 46.0, jnp.where(fat, 3.5, 5.0))
    sig_frozen = jnp.where(lean, 0.2, jnp.where(fat, 0.05, 0.1))
    sig_span = jnp.where(lean, 7.8, jnp.where(fat, 0.35, 0.9))
    eps2 = 2.0 * (eps_frozen + eps_span * frac)
    sigma = sig_frozen + sig_span * frac
    half = sigma * COURANT
    inv = 1.0 / (eps2 + half)
    return sigma, (eps2 - half) * inv, (2.0 * COURANT) * inv


def fields_kernel(nc, nh, e_hbm, h_hbm, t_hbm, g_hbm, e, h, power, tags, sigma, ca, cb, xp, zp, xm, zm, cm, cp,
                  load_sem, ssem, rsem):
    sx, sz = t_hbm.shape[0], t_hbm.shape[1]
    nk = t_hbm.shape[2] // 128
    c = lax.axis_index("col")
    g = lax.axis_index("hgt")
    has_cp, has_cm = c < nc - 1, c > 0
    has_hp, has_hm = g < nh - 1, g > 0

    def lanes(k):
        return pl.ds(k * 128, 128)

    def loads(which):
        out = []
        for k in range(nk):
            if which < 3:
                out.append(pltpu.make_async_copy(
                    e_hbm.at[which, :, :, lanes(k)], e.at[which, pl.ds(0, sx), pl.ds(0, sz), k, :], load_sem.at[which]))
            elif which < 6:
                out.append(pltpu.make_async_copy(
                    h_hbm.at[which - 3, :, :, lanes(k)], h.at[which - 3, pl.ds(1, sx), pl.ds(1, sz), k, :], load_sem.at[which]))
            elif which == 6:
                out.append(pltpu.make_async_copy(t_hbm.at[:, :, lanes(k)], power.at[:, :, k, :], load_sem.at[which]))
            else:
                out.append(pltpu.make_async_copy(g_hbm.at[:, :, lanes(k)], tags.at[:, :, k, :], load_sem.at[which]))
        return out

    all_loads = [loads(w) for w in range(8)]
    for group in all_loads:
        for copy in group:
            copy.start()

    plan = [
        (has_cm, (c - 1, g), has_cp, e.at[pl.ds(1, 2), 0, pl.ds(0, sz)], xp),
        (has_hm, (c, g - 1), has_hp, e.at[pl.ds(0, 2), pl.ds(0, sx), 0], zp),
        (has_cp, (c + 1, g), has_cm, h.at[pl.ds(1, 2), sx, pl.ds(1, sz)], xm),
        (has_hp, (c, g + 1), has_hm, h.at[pl.ds(0, 2), pl.ds(1, sx), sz], zm),
        (has_cp & has_hm, (c + 1, g - 1), has_cm & has_hp, e.at[0, sx - 1, 0], cm),
        (has_cm & has_hp, (c - 1, g + 1), has_cp & has_hm, e.at[2, 0, sz - 1], cp),
    ]

    barrier = pltpu.get_barrier_semaphore()
    for sends, device, _, _, _ in plan:
        @pl.when(sends)
        def _(device=device):
            pl.semaphore_signal(barrier, inc=1, device_id=device, device_id_type=MESH)
    zero_tile = jnp.zeros((8, 128), F32)
    for i in range(3):
        e[i, sx] = jnp.zeros((sz + 1, 8, 128), F32)
        h[i, 0] = jnp.zeros((sz + 1, 8, 128), F32)

    def clear(x, _):
        for i in range(3):
            e[i, x, sz] = zero_tile
            h[i, x + 1, 0] = zero_tile
        return 0

    lax.fori_loop(0, sx, clear, 0)
    peers = 0
    for sends, _, _, _, _ in plan:
        peers = peers + sends.astype(jnp.int32)
    pl.semaphore_wait(barrier, peers)

    def copies(t):
        out = []
        for j, (sends, device, receives, src, buf) in enumerate(plan):
            out.append((sends, receives, pltpu.make_async_remote_copy(
                src_ref=src, dst_ref=buf.at[t], send_sem=ssem.at[t, j], recv_sem=rsem.at[t, j],
                device_id=device, device_id_type=MESH)))
        return out

    def update_h(x, z0, n):
        zs, zn = pl.ds(z0, n), pl.ds(z0 + 1, n)
        ex, ey, ez = e[0, x, zs], e[1, x, zs], e[2, x, zs]
        ex_z, ey_z = e[0, x, zn], e[1, x, zn]
        ey_x, ez_x = e[1, x + 1, zs], e[2, x + 1, zs]
        dy_z = shifted_up(ez) - ez
        dy_x = shifted_up(ex) - ex
        h[0, x + 1, zn] = h[0, x + 1, zn] - COURANT * (dy_z - (ey_z - ey))
        h[1, x + 1, zn] = h[1, x + 1, zn] - COURANT * ((ex_z - ex) - (ez_x - ez))
        h[2, x + 1, zn] = h[2, x + 1, zn] - COURANT * ((ey_x - ey) - dy_x)

    def update_e(x, z0, n):
        zs, zn = pl.ds(z0, n), pl.ds(z0 + 1, n)
        hx, hy, hz = h[0, x + 1, zn], h[1, x + 1, zn], h[2, x + 1, zn]
        hx_z, hy_z = h[0, x + 1, zs], h[1, x + 1, zs]
        hy_x, hz_x = h[1, x, zn], h[2, x, zn]
        dy_z = hz - shifted_down(hz)
        dy_x = hx - shifted_down(hx)
        a, b = ca[x, zs], cb[x, zs]
        ex = a * e[0, x, zs] + b * (dy_z - (hy - hy_z))
        ey = a * e[1, x, zs] + b * ((hx - hx_z) - (hz - hz_x))
        ez = a * e[2, x, zs] + b * ((hy - hy_x) - dy_x)
        e[0, x, zs] = ex
        e[1, x, zs] = ey
        e[2, x, zs] = ez
        power[x, zs] = power[x, zs] + sigma[x, zs] * (ex * ex + ey * ey + ez * ez)

    def over(x_lo, x_hi, z_lo, z_hi, chunk, body):
        count = (z_hi - z_lo) // chunk

        def at(i, _):
            x = x_lo + i // count
            body(x, z_lo + (i % count) * chunk, chunk)
            return 0

        lax.fori_loop(0, (x_hi - x_lo) * count, at, 0)

    def set_coefficients(x, z0, n):
        zs = pl.ds(z0, n)
        s, a, b = coefficients(power[x, zs], tags[x, zs])
        sigma[x, zs] = s
        ca[x, zs] = a
        cb[x, zs] = b
        power[x, zs] = jnp.zeros((n, 8, 128), F32)

    def corrections(t):
        @pl.when(has_cp)
        def _():
            h[1, sx, pl.ds(1, sz)] = h[1, sx, pl.ds(1, sz)] + COURANT * xp[t, 1]
            h[2, sx, pl.ds(1, sz)] = h[2, sx, pl.ds(1, sz)] - COURANT * xp[t, 0]

        @pl.when(has_cm)
        def _():
            h[1, 0, pl.ds(1, sz)] = xm[t, 0] + COURANT * e[2, 0, pl.ds(0, sz)]
            h[2, 0, pl.ds(1, sz)] = xm[t, 1] - COURANT * e[1, 0, pl.ds(0, sz)]

        @pl.when(has_cm & has_hp)
        def _():
            h[1, 0, sz] = h[1, 0, sz] - COURANT * cm[t]

        def rows(x, _):
            @pl.when(has_hp)
            def _():
                h[0, x + 1, sz] = h[0, x + 1, sz] + COURANT * zp[t, 1, x]
                h[1, x + 1, sz] = h[1, x + 1, sz] - COURANT * zp[t, 0, x]

            @pl.when(has_hm)
            def _():
                h[0, x + 1, 0] = zm[t, 0, x] + COURANT * e[1, x, 0]
                h[1, x + 1, 0] = zm[t, 1, x] - COURANT * e[0, x, 0]
            return 0

        lax.fori_loop(0, sx, rows, 0)

        @pl.when(has_cp & has_hm)
        def _():
            h[1, sx, 0] = h[1, sx, 0] + COURANT * cp[t]

    for w in range(6):
        for copy in all_loads[w]:
            copy.wait()
    for t in range(STEPS):
        over(sx - 1, sx, 0, sz, 4, update_h)
        over(0, sx - 1, sz - 1, sz, 1, update_h)
        for sends, _, copy in copies(t):
            pl.when(sends)(copy.start)
        over(0, sx - 1, 0, sz - 2, 2, update_h)
        over(0, sx - 1, sz - 2, sz - 1, 1, update_h)
        if t == 0:
            for w in range(6, 8):
                for copy in all_loads[w]:
                    copy.wait()
            over(0, sx, 0, sz, 4, set_coefficients)
        over(1, sx - 1, 1, sz - 1, 2, update_e)
        for sends, receives, copy in copies(t):
            pl.when(sends)(copy.wait_send)
            pl.when(receives)(copy.wait_recv)
        corrections(t)
        over(0, 1, 0, sz, 2, update_e)
        over(sx - 1, sx, 0, sz, 2, update_e)
        over(1, sx - 1, 0, 1, 1, update_e)
        over(1, sx - 1, sz - 1, sz, 1, update_e)


def route_kernel(n_dev, cap, owner_ref, node_ref, where_ref, nodes_ref):
    rows = owner_ref.shape[0]
    who = lax.broadcasted_iota(jnp.int32, (n_dev, 128), 0)
    earlier = (lax.broadcasted_iota(jnp.int32, (128, 128), 0) < lax.broadcasted_iota(jnp.int32, (128, 128), 1)).astype(jnp.bfloat16)
    slot = lax.broadcasted_iota(jnp.int32, (128, 128), 0)
    base = jnp.zeros((n_dev, 1), F32)
    hi = jnp.zeros((n_dev, 128), F32)
    lo = jnp.zeros((n_dev, 128), F32)
    for r in range(rows):
        own = owner_ref[pl.ds(r, 1), :]
        node = node_ref[pl.ds(r, 1), :] + 1
        hit = who == own
        hit_f = hit.astype(F32)
        hit_b = hit_f.astype(jnp.bfloat16)
        before = jnp.dot(hit_b, earlier, preferred_element_type=F32) + base
        rank = jnp.sum(hit_f * before, axis=0, keepdims=True).astype(jnp.int32)
        base = base + jnp.sum(hit_f, axis=1, keepdims=True)
        where_ref[pl.ds(r, 1), :] = own * cap + rank
        at = slot == rank
        node_hi = (node // 16).astype(F32)
        node_lo = (node % 16).astype(F32)
        dims = (((1,), (1,)), ((), ()))
        hi = hi + lax.dot_general(hit_b, jnp.where(at, node_hi, 0.0).astype(jnp.bfloat16), dims, preferred_element_type=F32)
        lo = lo + lax.dot_general(hit_b, jnp.where(at, node_lo, 0.0).astype(jnp.bfloat16), dims, preferred_element_type=F32)
    nodes_ref[...] = (16.0 * hi + lo).reshape(nodes_ref.shape)


def pack_kernel(where_ref, e, h, power, e_hbm, h_hbm, slots, sem):
    sx, sz = power.shape[0], power.shape[1]
    nk = e_hbm.shape[3] // 128
    copies = []
    for i in range(3):
        for k in range(nk):
            copies.append(pltpu.make_async_copy(
                e.at[i, pl.ds(0, sx), pl.ds(0, sz), k, :], e_hbm.at[i, :, :, pl.ds(k * 128, 128)], sem.at[0]))
            copies.append(pltpu.make_async_copy(
                h.at[i, pl.ds(1, sx), pl.ds(1, sz), k, :], h_hbm.at[i, :, :, pl.ds(k * 128, 128)], sem.at[0]))
    for copy in copies:
        copy.start()
    chunk = 64

    def clear(i, _):
        slots[pl.ds(i * chunk, chunk)] = jnp.zeros((chunk, 1, 128), F32)
        return 0

    lax.fori_loop(0, slots.shape[0] // chunk, clear, 0)

    def place(i, _):
        x, z2 = i // (sz // 2), i % (sz // 2)
        for dz in range(2):
            tile = power[x, z2 * 2 + dz] * (1.0 / STEPS)
            for k in range(nk):
                row = i * 2 * nk + dz * nk + k
                slots[where_ref[row // 128, row % 128]] = tile[k : k + 1, :]
        return 0

    lax.fori_loop(0, sx * sz // 2, place, 0)
    for copy in copies:
        copy.wait()


def deposit_kernel(nc, nh, cap, slots, nodes, enthalpy, out, recv, recv_nodes, ssem, rsem, nsem, msem, lsem):
    n_dev = nc * nh
    c = lax.axis_index("col")
    g = lax.axis_index("hgt")
    me = c * nh + g
    barrier = pltpu.get_barrier_semaphore()

    def partner(d):
        t = me ^ ((d * 37) % n_dev)
        return t, (t // nh, t % nh)

    def greet(d, _):
        pl.semaphore_signal(barrier, inc=1, device_id=partner(d)[1], device_id_type=MESH)
        return 0

    lax.fori_loop(1, n_dev, greet, 0)
    own = pltpu.make_async_copy(slots.at[me], recv.at[me], lsem.at[0])
    own_nodes = pltpu.make_async_copy(nodes.at[me], recv_nodes.at[me], lsem.at[1])
    own.start()
    own_nodes.start()
    pl.semaphore_wait(barrier, n_dev - 1)

    def send(d, _):
        t, device = partner(d)
        pltpu.make_async_remote_copy(nodes.at[t], recv_nodes.at[me], nsem, msem, device_id=device, device_id_type=MESH).start()
        pltpu.make_async_remote_copy(slots.at[t], recv.at[me], ssem, rsem, device_id=device, device_id_type=MESH).start()
        return 0

    lax.fori_loop(1, n_dev, send, 0)
    own.wait()
    own_nodes.wait()
    others = pl.ds(0, n_dev - 1)
    pltpu.make_async_copy(nodes.at[others], recv_nodes.at[others], msem).wait()
    pltpu.make_async_copy(slots.at[others], recv.at[others], rsem).wait()
    n_nodes = enthalpy.shape[0]
    group = 8
    count = lax.broadcasted_iota(jnp.int32, (n_nodes, group * cap), 0).astype(F32) + 1.0

    def add(i, heat):
        rows = recv[pl.ds(i * group, group)].reshape(group * cap, 128)
        high = rows.astype(jnp.bfloat16)
        low = (rows - high.astype(F32)).astype(jnp.bfloat16)
        tags = recv_nodes[pl.ds(i * group, group)]
        tags = jnp.concatenate([tags[s][:, :cap] for s in range(group)], axis=1)
        pick = jnp.where(count == tags, 1.0, 0.0).astype(jnp.bfloat16)
        both = jnp.dot(pick, jnp.concatenate([high, low], axis=1), preferred_element_type=F32)
        return heat + (both[:, :128] + both[:, 128:])

    heat = lax.fori_loop(0, n_dev // group, add, jnp.zeros((n_nodes, 128), F32))
    q = enthalpy[...] + 0.25 * heat
    out[...] = jnp.where(q < 0.0, q / 2.0, jnp.where(q > 1.0, (q - 1.0) / 3.0, 0.0))
    pltpu.make_async_copy(nodes.at[others], recv_nodes.at[others], nsem).wait()
    pltpu.make_async_copy(slots.at[others], recv.at[others], ssem).wait()


def per_device(nc, nh, efield, hfield, cell_temp, region_tags, block_owner, block_node, node_enthalpy):
    sx, sz, sy = cell_temp.shape
    n_dev = nc * nh
    blocks = sx * sz * sy // 128
    cap = 2 * blocks // n_dev
    dma = pltpu.SemaphoreType.DMA

    def tiles(*shape):
        return pltpu.VMEM(shape + (8, 128), F32)

    def out(*shape):
        return jax.ShapeDtypeStruct(shape, F32)

    where_to, nodes = pl.pallas_call(
        lambda *refs: route_kernel(n_dev, cap, *refs),
        out_shape=(jax.ShapeDtypeStruct((blocks // 128, 128), jnp.int32), out(n_dev, 1, 128)),
        in_specs=[VMEM] * 2,
        out_specs=(VMEM, VMEM),
        name="route",
    )(block_owner.reshape(-1, 128), block_node.reshape(-1, 128))
    e, h, power = pl.pallas_call(
        lambda *refs: fields_kernel(nc, nh, *refs),
        out_shape=(tiles(3, sx + 1, sz + 1), tiles(3, sx + 1, sz + 1), tiles(sx, sz)),
        in_specs=[HBM] * 4,
        out_specs=(VMEM, VMEM, VMEM),
        scratch_shapes=[
            pltpu.VMEM((sx, sz, 8, 128), jnp.int32), tiles(sx, sz), tiles(sx, sz), tiles(sx, sz),
            tiles(STEPS, 2, sz), tiles(STEPS, 2, sx), tiles(STEPS, 2, sz), tiles(STEPS, 2, sx), tiles(STEPS), tiles(STEPS),
            dma((8,)), dma((STEPS, 6)), dma((STEPS, 6)),
        ],
        compiler_params=pltpu.CompilerParams(collective_id=0, has_side_effects=True, vmem_limit_bytes=28 << 20),
        name="fields",
    )(efield, hfield, cell_temp, region_tags)
    e_out, h_out, slots = pl.pallas_call(
        pack_kernel,
        out_shape=(out(3, sx, sz, sy), out(3, sx, sz, sy), out(n_dev * cap, 1, 128)),
        in_specs=[SMEM, VMEM, VMEM, VMEM],
        out_specs=(HBM, HBM, VMEM),
        scratch_shapes=[dma((1,))],
        compiler_params=pltpu.CompilerParams(vmem_limit_bytes=24 << 20),
        name="pack",
    )(where_to, e, h, power)
    temp = pl.pallas_call(
        lambda *refs: deposit_kernel(nc, nh, cap, *refs),
        out_shape=out(*node_enthalpy.shape),
        in_specs=[ANY, ANY, VMEM],
        out_specs=VMEM,
        scratch_shapes=[
            pltpu.VMEM((n_dev, cap, 128), F32), pltpu.VMEM((n_dev, 1, 128), F32), dma, dma, dma, dma, dma((2,)),
        ],
        compiler_params=pltpu.CompilerParams(collective_id=1, has_side_effects=True, vmem_limit_bytes=16 << 20),
        name="deposit",
    )(slots.reshape(n_dev, cap, 128), nodes, node_enthalpy)
    return e_out, h_out, temp


def solution(mesh):
    placed = (
        P(None, "col", "hgt", None),
        P(None, "col", "hgt", None),
        P("col", "hgt", None),
        P("col", "hgt", None),
        P("col", "hgt", None, None, None, None),
        P("col", "hgt", None, None, None),
        P(("col", "hgt"), None),
    )
    nc, nh = mesh.shape["col"], mesh.shape["hgt"]
    return jax.shard_map(
        lambda *args: per_device(nc, nh, *args),
        mesh=mesh,
        in_specs=placed,
        out_specs=(P(None, "col", "hgt", None), P(None, "col", "hgt", None), P(("col", "hgt"), None)),
        check_vma=False,
    )
```

time: 304 us -> 249 us (0.82); the launches traced: 299 us -> 248 us
  Pallas kernels: 0 us -> 236 us
  other arithmetic: 104 us -> 0 us
  starting transfers between devices: 73.1 us -> 0 us
  waiting for transfers between devices: 56.2 us -> 0 us
  local copies, waits for them, and re-layouts: 54.7 us -> 11.5 us
  matrix products: 9.01 us -> 0 us
    pallas_call x0 -> x4, Pallas kernels: none -> 236 us  [the longest x1 148 us: per_device(): pl.pallas_call(lambda *refs: fields_kernel(nc, nh, *refs), out_shape=(til...]
    ppermute x16 -> x0, starting transfers between devices: 44.5 us -> none  [from_behind(): return lax.ppermute(block, axis, route)]
    all_to_all x2 -> x0, waiting for transfers between devices: 38.7 us -> none  [the longest x1 38.7 us: per_device(): lax.all_to_all(send_vals, ('col', 'hgt'), split_axis=0, concat_axis=0, ti...]
    another operation x10 -> x0, other arithmetic: 34.7 us -> none  [the longest x8 34.2 us: curl(): return jnp.stack([dy_z - dz_y, dz_x - dx_z, dx_y - dy_x])]
    all_to_all x2 -> x0, starting transfers between devices: 28.7 us -> none  [the longest x1 16.5 us: per_device(): lax.all_to_all(send_vals, ('col', 'hgt'), split_axis=0, concat_axis=0, ti...]
    add x4 -> x0, other arithmetic: 24.2 us -> none  [per_device(): ca * efield_lattice_vector]
    scatter x2 -> x0, local copies, waits for them, and re-layouts: 22.1 us -> none  [the longest x1 11.8 us: per_device(): jnp.full((n_dev * capacity,), -1.0, jnp.float32).at[where_to].set(nodes)]
    slice x44 -> x0, local copies, waits for them, and re-layouts: 17.7 us -> none  [the longest x16 9.18 us: forward(): lax.slice_in_dim(field, 1, size, axis=axis)]
  transfers between devices with their start and end apart: 18 -> 0, of which waited for: 9 -> 0; matrix products, arithmetic and copies ran while one was open for 51% -> 0% of each run, Pallas kernels for 0% -> 0%
where the time goes in v1:
time: 249 us; the launch traced here: 248 us
  Pallas kernels  236 us (95%)
  local copies, waits for them, and re-layouts  11.5 us (5%)
    pallas_call x1, Pallas kernels, per_device(): pl.pallas_call(lambda *refs: fields_kernel(nc, nh, *refs), out_shape=(til...  148 us
    pallas_call x1, Pallas kernels, per_device(): pl.pallas_call(lambda *refs: deposit_kernel(nc, nh, cap, *refs), out_shap...  55 us
    pallas_call x1, Pallas kernels, per_device(): pl.pallas_call(pack_kernel, out_shape=(out(3, sx, sz, sy), out(3, sx, sz,...  26.8 us
    unnamed x17, local copies, waits for them, and re-layouts  10.1 us
    pallas_call x1, Pallas kernels, per_device(): pl.pallas_call(lambda *refs: route_kernel(n_dev, cap, *refs), out_shape=(...  6.29 us

profile of v1, /device:TPU:1, one launch (start us, length us, event | category | flops | bytes accessed | tf_op | source)
XLA Modules:
  0.0 248.4 jit_solution(10498629972747167169)
XLA Ops:
  0.6 0.9 copy.12
  1.6 0.7 reshape.15.refs_0_
  2.3 0.9 copy.13
  3.3 0.7 reshape.16.refs_1_
  4.0 6.3 %route.1 = (s32[24,128]{1,0:T(8,128)}, f32[128,1,128]{2,1,0:T(1,128)}) custom-call(s32[24,128]{1,0:T(8,128)} %reshape.15.refs_0_, s32[24,128]{1,0:T(8,128)} %reshape.16.refs_1_), custom_call_target="tpu_custom_call" | custom-call | tf_op jit(solution)/shard_map/route/pallas_call | solution.py:355
  10.3 0.0 copy-start
  10.3 2.3 copy-done
  12.6 0.0 copy-start.1
  12.6 2.3 copy-done.1
  15.0 0.0 copy-start.2
  15.0 1.4 copy-done.2
  16.4 0.0 copy-start.3
  16.4 1.4 copy-done.3
  17.8 0.0 copy-start.6
  17.8 148.1 %fields.1 = (f32[3,17,25,8,128]{4,3,2,1,0:T(8,128)S(1)}, f32[3,17,25,8,128]{4,3,2,1,0:T(8,128)S(1)}, f32[16,24,8,128]{3,2,1,0:T(8,128)S(1)}) custom-call(f32[3,16,24,1024]{3,2,1,0:T(8,128)S(1)} %copy-done, f32[3,16,24,1024]{3,2,1,0:T(8,128)S(1)} %copy-done.1, f32[16,24,1024]{2,1,0:T(8,128)S(1)} %copy-done.2, s32[16,24,1024]{2,1,0:T(8,128)S(1)} %copy-done.3), custom_call_target="tpu_custom_call" | custom-call | tf_op jit(solution)/shard_map/fields/pallas_call | solution.py:362
  165.8 0.0 copy-done.6
  165.9 0.0 copy-start.4
  165.9 0.0 copy-start.5
  165.9 26.8 %pack.1 = (f32[3,16,24,1024]{3,2,1,0:T(8,128)}, f32[3,16,24,1024]{3,2,1,0:T(8,128)}, f32[6144,1,128]{2,1,0:T(1,128)S(1)}) custom-call(s32[24,128]{1,0:T(8,128)S(1)} %copy-done.6, f32[3,17,25,8,128]{4,3,2,1,0:T(8,128)S(1)} %get-tuple-element.12.e, f32[3,17,25,8,128]{4,3,2,1,0:T(8,128)S(1)} %get-tuple-element.13.h, f32[16,24,8,128]{3,2,1,0:T(8,128)S(1)} %get-tuple-element.14.power), custom_call_target="tpu_custom_call" | custom-call | tf_op jit(solution)/shard_map/pack/pallas_call | solution.py:375
  192.7 0.0 copy-done.4
  192.7 0.0 copy-done.5
  192.8 55.0 %deposit.1 = f32[384,128]{1,0:T(8,128)S(1)} custom-call(f32[128,48,128]{2,1,0:T(8,128)S(1)} %bitcast.7, f32[128,1,128]{2,1,0:T(1,128)S(1)} %copy-done.5, f32[384,128]{1,0:T(8,128)S(1)} %copy-done.4), custom_call_target="tpu_custom_call" | custom-call | tf_op jit(solution)/shard_map/deposit/pallas_call | solution.py:384
  247.8 0.7 copy.15
Async XLA Ops:
  10.3 2.3 copy-start
  12.6 2.3 copy-start.1
  15.0 1.4 copy-start.2
  16.4 1.4 copy-start.3
  17.8 148.1 %copy-start.6 = (s32[24,128]{1,0:T(8,128)S(1)}, s32[24,128]{1,0:T(8,128)}, u32[]{:S(2)}) copy-start(s32[24,128]{1,0:T(8,128)} %get-tuple-element.11.where_ref) | copy-start | bytes 36868
  165.9 26.9 %copy-start.4 = (f32[384,128]{1,0:T(8,128)S(1)}, f32[384,128]{1,0:T(8,128)}, u32[]{:S(2)}) copy-start(f32[384,128]{1,0:T(8,128)} %refs_2_.3) | copy-start | bytes 589828
  165.9 26.9 %copy-start.5 = (f32[128,1,128]{2,1,0:T(1,128)S(1)}, f32[128,1,128]{2,1,0:T(1,128)}, u32[]{:S(2)}) copy-start(f32[128,1,128]{2,1,0:T(1,128)} %get-tuple-element.18.refs_1_) | copy-start | bytes 196612

commit v2 on v1

--- a/solution.py
+++ b/solution.py
@@ -7,6 +7,8 @@
 
 STEPS = 4
 COURANT = 0.55
+NXH = 1
+NXE = 1
 MESH = pl.DeviceIdType.MESH
 F32 = jnp.float32
 ANY = pl.BlockSpec(memory_space=pl.ANY)
@@ -119,50 +121,50 @@
                 device_id=device, device_id_type=MESH)))
         return out
 
-    def update_h(x, z0, n):
-        zs, zn = pl.ds(z0, n), pl.ds(z0 + 1, n)
-        ex, ey, ez = e[0, x, zs], e[1, x, zs], e[2, x, zs]
-        ex_z, ey_z = e[0, x, zn], e[1, x, zn]
-        ey_x, ez_x = e[1, x + 1, zs], e[2, x + 1, zs]
-        dy_z = shifted_up(ez) - ez
-        dy_x = shifted_up(ex) - ex
-        h[0, x + 1, zn] = h[0, x + 1, zn] - COURANT * (dy_z - (ey_z - ey))
-        h[1, x + 1, zn] = h[1, x + 1, zn] - COURANT * ((ex_z - ex) - (ez_x - ez))
-        h[2, x + 1, zn] = h[2, x + 1, zn] - COURANT * ((ey_x - ey) - dy_x)
-
-    def update_e(x, z0, n):
-        zs, zn = pl.ds(z0, n), pl.ds(z0 + 1, n)
-        hx, hy, hz = h[0, x + 1, zn], h[1, x + 1, zn], h[2, x + 1, zn]
-        hx_z, hy_z = h[0, x + 1, zs], h[1, x + 1, zs]
-        hy_x, hz_x = h[1, x, zn], h[2, x, zn]
-        dy_z = hz - shifted_down(hz)
-        dy_x = hx - shifted_down(hx)
-        a, b = ca[x, zs], cb[x, zs]
-        ex = a * e[0, x, zs] + b * (dy_z - (hy - hy_z))
-        ey = a * e[1, x, zs] + b * ((hx - hx_z) - (hz - hz_x))
-        ez = a * e[2, x, zs] + b * ((hy - hy_x) - dy_x)
-        e[0, x, zs] = ex
-        e[1, x, zs] = ey
-        e[2, x, zs] = ez
-        power[x, zs] = power[x, zs] + sigma[x, zs] * (ex * ex + ey * ey + ez * ez)
-
-    def over(x_lo, x_hi, z_lo, z_hi, chunk, body):
-        count = (z_hi - z_lo) // chunk
-
+    def update_h(x, nx, z0, nz):
+        xs, xn, zs, zn, zw = pl.ds(x, nx), pl.ds(x + 1, nx), pl.ds(z0, nz), pl.ds(z0 + 1, nz), pl.ds(z0, nz + 1)
+        ex, ey, ez = e[0, xs, zw], e[1, xs, zw], e[2, xs, zs]
+        ey_x, ez_x = e[1, xn, zs], e[2, xn, zs]
+        hx, hy, hz = h[0, xn, zn], h[1, xn, zn], h[2, xn, zn]
+        ex, ex_z = ex[:, :nz], ex[:, 1:]
+        ey, ey_z = ey[:, :nz], ey[:, 1:]
+        hx = hx - COURANT * ((shifted_up(ez) - ez) - (ey_z - ey))
+        hy = hy - COURANT * ((ex_z - ex) - (ez_x - ez))
+        hz = hz - COURANT * ((ey_x - ey) - (shifted_up(ex) - ex))
+        h[0, xn, zn] = hx
+        h[1, xn, zn] = hy
+        h[2, xn, zn] = hz
+
+    def update_e(x, nx, z0, nz):
+        xs, xn, zs, zn, zw = pl.ds(x, nx), pl.ds(x + 1, nx), pl.ds(z0, nz), pl.ds(z0 + 1, nz), pl.ds(z0, nz + 1)
+        hx, hy, hz = h[0, xn, zw], h[1, xn, zw], h[2, xn, zn]
+        hy_x, hz_x = h[1, xs, zn], h[2, xs, zn]
+        ex, ey, ez = e[0, xs, zs], e[1, xs, zs], e[2, xs, zs]
+        a, b, s, p = ca[xs, zs], cb[xs, zs], sigma[xs, zs], power[xs, zs]
+        hx_z, hx = hx[:, :nz], hx[:, 1:]
+        hy_z, hy = hy[:, :nz], hy[:, 1:]
+        ex = a * ex + b * ((hz - shifted_down(hz)) - (hy - hy_z))
+        ey = a * ey + b * ((hx - hx_z) - (hz - hz_x))
+        ez = a * ez + b * ((hy - hy_x) - (hx - shifted_down(hx)))
+        e[0, xs, zs] = ex
+        e[1, xs, zs] = ey
+        e[2, xs, zs] = ez
+        power[xs, zs] = p + s * (ex * ex + ey * ey + ez * ez)
+
+    def over(x_lo, x_hi, nx, z_lo, z_hi, body):
         def at(i, _):
-            x = x_lo + i // count
-            body(x, z_lo + (i % count) * chunk, chunk)
+            body(x_lo + i * nx, nx, z_lo, z_hi - z_lo)
             return 0
 
-        lax.fori_loop(0, (x_hi - x_lo) * count, at, 0)
-
-    def set_coefficients(x, z0, n):
-        zs = pl.ds(z0, n)
-        s, a, b = coefficients(power[x, zs], tags[x, zs])
-        sigma[x, zs] = s
-        ca[x, zs] = a
-        cb[x, zs] = b
-        power[x, zs] = jnp.zeros((n, 8, 128), F32)
+        lax.fori_loop(0, (x_hi - x_lo) // nx, at, 0)
+
+    def set_coefficients(x, nx, z0, nz):
+        xs, zs = pl.ds(x, nx), pl.ds(z0, nz)
+        s, a, b = coefficients(power[xs, zs], tags[xs, zs])
+        sigma[xs, zs] = s
+        ca[xs, zs] = a
+        cb[xs, zs] = b
+        power[xs, zs] = jnp.zeros((nx, nz, 8, 128), F32)
 
     def corrections(t):
         @pl.when(has_cp)
@@ -201,26 +203,25 @@
         for copy in all_loads[w]:
             copy.wait()
     for t in range(STEPS):
-        over(sx - 1, sx, 0, sz, 4, update_h)
-        over(0, sx - 1, sz - 1, sz, 1, update_h)
+        update_h(sx - 1, 1, 0, sz)
+        update_h(0, sx - 1, sz - 1, 1)
         for sends, _, copy in copies(t):
             pl.when(sends)(copy.start)
-        over(0, sx - 1, 0, sz - 2, 2, update_h)
-        over(0, sx - 1, sz - 2, sz - 1, 1, update_h)
+        over(0, sx - 1, NXH, 0, sz - 1, update_h)
         if t == 0:
             for w in range(6, 8):
                 for copy in all_loads[w]:
                     copy.wait()
-            over(0, sx, 0, sz, 4, set_coefficients)
-        over(1, sx - 1, 1, sz - 1, 2, update_e)
+            over(0, sx, 1, 0, sz, set_coefficients)
+        over(1, sx - 1, NXE, 1, sz - 1, update_e)
         for sends, receives, copy in copies(t):
             pl.when(sends)(copy.wait_send)
             pl.when(receives)(copy.wait_recv)
         corrections(t)
-        over(0, 1, 0, sz, 2, update_e)
-        over(sx - 1, sx, 0, sz, 2, update_e)
-        over(1, sx - 1, 0, 1, 1, update_e)
-        over(1, sx - 1, sz - 1, sz, 1, update_e)
+        update_e(0, 1, 0, sz)
+        update_e(sx - 1, 1, 0, sz)
+        update_e(1, sx - 2, 0, 1)
+        update_e(1, sx - 2, sz - 1, 1)
 
 
 def route_kernel(n_dev, cap, owner_ref, node_ref, where_ref, nodes_ref):
@@ -251,7 +252,7 @@
 
 
 def pack_kernel(where_ref, e, h, power, e_hbm, h_hbm, slots, sem):
-    sx, sz = power.shape[0], power.shape[1]
+    sx, sz = e_hbm.shape[1], e_hbm.shape[2]
     nk = e_hbm.shape[3] // 128
     copies = []
     for i in range(3):
@@ -270,16 +271,16 @@
 
     lax.fori_loop(0, slots.shape[0] // chunk, clear, 0)
 
+    tiles = where_ref.shape[1] // nk
+
     def place(i, _):
-        x, z2 = i // (sz // 2), i % (sz // 2)
-        for dz in range(2):
-            tile = power[x, z2 * 2 + dz] * (1.0 / STEPS)
+        for j in range(tiles):
+            tile = power[i * tiles + j] * (1.0 / STEPS)
             for k in range(nk):
-                row = i * 2 * nk + dz * nk + k
-                slots[where_ref[row // 128, row % 128]] = tile[k : k + 1, :]
+                slots[where_ref[i, j * nk + k]] = tile[k : k + 1, :]
         return 0
 
-    lax.fori_loop(0, sx * sz // 2, place, 0)
+    lax.fori_loop(0, where_ref.shape[0], place, 0)
     for copy in copies:
         copy.wait()
 
@@ -369,7 +370,7 @@
             tiles(STEPS, 2, sz), tiles(STEPS, 2, sx), tiles(STEPS, 2, sz), tiles(STEPS, 2, sx), tiles(STEPS), tiles(STEPS),
             dma((8,)), dma((STEPS, 6)), dma((STEPS, 6)),
         ],
-        compiler_params=pltpu.CompilerParams(collective_id=0, has_side_effects=True, vmem_limit_bytes=28 << 20),
+        compiler_params=pltpu.CompilerParams(collective_id=0, has_side_effects=True, vmem_limit_bytes=48 << 20),
         name="fields",
     )(efield, hfield, cell_temp, region_tags)
     e_out, h_out, slots = pl.pallas_call(
@@ -380,7 +381,7 @@
         scratch_shapes=[dma((1,))],
         compiler_params=pltpu.CompilerParams(vmem_limit_bytes=24 << 20),
         name="pack",
-    )(where_to, e, h, power)
+    )(where_to, e, h, power.reshape(sx * sz, 8, 128))
     temp = pl.pallas_call(
         lambda *refs: deposit_kernel(nc, nh, cap, *refs),
         out_shape=out(*node_enthalpy.shape),

time: 249 us -> 104 us (0.42)
  Pallas kernels: 236 us -> 99.2 us
  local copies, waits for them, and re-layouts: 11.5 us -> 4.05 us
    pallas_call x1, Pallas kernels: 148 us -> 31.2 us  [per_device(): pl.pallas_call(lambda *refs: fields_kernel(nc, nh, *refs), out_shape=(til...]
    pallas_call x1, Pallas kernels: 26.8 us -> 5.32 us  [per_device(): pl.pallas_call(pack_kernel, out_shape=(out(3, sx, sz, sy), out(3, sx, sz,...]
    unnamed x17 -> x9, local copies, waits for them, and re-layouts: 10.1 us -> 2.58 us
where the time goes in v2:
time: 104 us
  Pallas kernels  99.2 us (95%)
  local copies, waits for them, and re-layouts  4.05 us (4%)
    pallas_call x1, Pallas kernels, per_device(): pl.pallas_call(lambda *refs: deposit_kernel(nc, nh, cap, *refs), out_shap...  56.4 us
    pallas_call x1, Pallas kernels, per_device(): pl.pallas_call(lambda *refs: fields_kernel(nc, nh, *refs), out_shape=(til...  31.2 us
    pallas_call x1, Pallas kernels, per_device(): pl.pallas_call(lambda *refs: route_kernel(n_dev, cap, *refs), out_shape=(...  6.29 us
    pallas_call x1, Pallas kernels, per_device(): pl.pallas_call(pack_kernel, out_shape=(out(3, sx, sz, sy), out(3, sx, sz,...  5.32 us
    unnamed x9, local copies, waits for them, and re-layouts  2.58 us

profile of v2, /device:TPU:1, one launch (start us, length us, event | category | flops | bytes accessed | tf_op | source)
XLA Modules:
  0.0 104.0 jit_solution(3713874345909622739)
XLA Ops:
  0.6 0.9 copy.12
  1.6 0.7 reshape.18.refs_0_
  2.3 0.9 copy.13
  3.3 0.7 reshape.19.refs_1_
  4.0 6.3 %route.1 = (s32[24,128]{1,0:T(8,128)}, f32[128,1,128]{2,1,0:T(1,128)}) custom-call(s32[24,128]{1,0:T(8,128)} %reshape.18.refs_0_, s32[24,128]{1,0:T(8,128)} %reshape.19.refs_1_), custom_call_target="tpu_custom_call" | custom-call | tf_op jit(solution)/shard_map/route/pallas_call | solution.py:356
  10.3 0.0 copy-start.2
  10.3 31.2 %fields.1 = (f32[3,17,25,8,128]{4,3,2,1,0:T(8,128)S(1)}, f32[3,17,25,8,128]{4,3,2,1,0:T(8,128)S(1)}, f32[16,24,8,128]{3,2,1,0:T(8,128)S(1)}) custom-call(f32[3,16,24,1024]{3,2,1,0:T(8,128)} %refs_0_.1, f32[3,16,24,1024]{3,2,1,0:T(8,128)} %refs_1_.1, f32[16,24,1024]{2,1,0:T(8,128)} %refs_2_.2, s32[16,24,1024]{2,1,0:T(8,128)} %refs_3_.1), custom_call_target="tpu_custom_call" | custom-call | tf_op jit(solution)/shard_map/fields/pallas_call | solution.py:363
  41.5 0.0 copy-done.2
  41.5 0.0 copy-start
  41.5 0.0 copy-start.1
  41.5 5.3 %pack.1 = (f32[3,16,24,1024]{3,2,1,0:T(8,128)}, f32[3,16,24,1024]{3,2,1,0:T(8,128)}, f32[6144,1,128]{2,1,0:T(1,128)S(1)}) custom-call(s32[24,128]{1,0:T(8,128)S(1)} %copy-done.2, f32[3,17,25,8,128]{4,3,2,1,0:T(8,128)S(1)} %get-tuple-element.12.e, f32[3,17,25,8,128]{4,3,2,1,0:T(8,128)S(1)} %get-tuple-element.13.h, f32[384,8,128]{2,1,0:T(8,128)S(1)} %bitcast.9), custom_call_target="tpu_custom_call" | custom-call | tf_op jit(solution)/shard_map/pack/pallas_call | solution.py:376
  46.9 0.0 copy-done
  46.9 0.0 copy-done.1
  46.9 56.4 %deposit.1 = f32[384,128]{1,0:T(8,128)S(1)} custom-call(f32[128,48,128]{2,1,0:T(8,128)S(1)} %bitcast.8, f32[128,1,128]{2,1,0:T(1,128)S(1)} %copy-done.1, f32[384,128]{1,0:T(8,128)S(1)} %copy-done), custom_call_target="tpu_custom_call" | custom-call | tf_op jit(solution)/shard_map/deposit/pallas_call | solution.py:385
  103.3 0.7 copy.15
Async XLA Ops:
  10.3 31.2 %copy-start.2 = (s32[24,128]{1,0:T(8,128)S(1)}, s32[24,128]{1,0:T(8,128)}, u32[]{:S(2)}) copy-start(s32[24,128]{1,0:T(8,128)} %get-tuple-element.11.where_ref) | copy-start | bytes 36868
  41.5 5.4 %copy-start = (f32[384,128]{1,0:T(8,128)S(1)}, f32[384,128]{1,0:T(8,128)}, u32[]{:S(2)}) copy-start(f32[384,128]{1,0:T(8,128)} %refs_2_.3) | copy-start | bytes 589828
  41.5 5.4 %copy-start.1 = (f32[128,1,128]{2,1,0:T(1,128)S(1)}, f32[128,1,128]{2,1,0:T(1,128)}, u32[]{:S(2)}) copy-start(f32[128,1,128]{2,1,0:T(1,128)} %get-tuple-element.18.refs_1_) | copy-start | bytes 196612

commit v3 on v2

v3 whole, which is shorter than its diff:
```python
import jax
import jax.numpy as jnp
from jax import lax
from jax.experimental import pallas as pl
from jax.experimental.pallas import tpu as pltpu
from jax.sharding import PartitionSpec as P

STEPS = 4
COURANT = 0.55
NXH = 1
NXE = 1
GROUP = 8
MESH = pl.DeviceIdType.MESH
F32 = jnp.float32
HBM = pl.BlockSpec(memory_space=pltpu.HBM)
VMEM = pl.BlockSpec(memory_space=pltpu.VMEM)
SMEM = pl.BlockSpec(memory_space=pltpu.SMEM)


def shifted_up(f):
    axis = f.ndim - 1
    lane = lax.broadcasted_iota(jnp.int32, f.shape, axis)
    sub = lax.broadcasted_iota(jnp.int32, f.shape, axis - 1)
    r = pltpu.roll(f, 127, axis)
    u = pltpu.roll(r, 7, axis - 1)
    return jnp.where(lane < 127, r, jnp.where(sub < 7, u, 0.0))


def shifted_down(f):
    axis = f.ndim - 1
    lane = lax.broadcasted_iota(jnp.int32, f.shape, axis)
    sub = lax.broadcasted_iota(jnp.int32, f.shape, axis - 1)
    r = pltpu.roll(f, 1, axis)
    u = pltpu.roll(r, 1, axis - 1)
    return jnp.where(lane > 0, r, jnp.where(sub > 0, u, 0.0))


def coefficients(temp, tags):
    frac = 1.0 / (1.0 + jnp.exp(-2.0 * temp))
    lean = tags == 0
    fat = tags == 1
    eps_frozen = jnp.where(lean, 4.0, jnp.where(fat, 2.5, 5.0))
    eps_span = jnp.where(lean, 46.0, jnp.where(fat, 3.5, 5.0))
    sig_frozen = jnp.where(lean, 0.2, jnp.where(fat, 0.05, 0.1))
    sig_span = jnp.where(lean, 7.8, jnp.where(fat, 0.35, 0.9))
    eps2 = 2.0 * (eps_frozen + eps_span * frac)
    sigma = sig_frozen + sig_span * frac
    half = sigma * COURANT
    inv = 1.0 / (eps2 + half)
    return sigma, (eps2 - half) * inv, (2.0 * COURANT) * inv


def fields_kernel(nc, nh, cap, source, e_hbm, h_hbm, t_hbm, g_hbm, nodes, enthalpy, e, h, out,
                  power, tags, sigma, ca, cb, xp, zp, xm, zm, cm, cp, send, recv, recv_nodes,
                  load_sem, ssem, rsem, ready, local_sem, out_sem, in_sem, node_out_sem, node_in_sem):
    n_dev = nc * nh
    sx, sz = t_hbm.shape[0], t_hbm.shape[1]
    nk = t_hbm.shape[2] // 128
    c = lax.axis_index("col")
    g = lax.axis_index("hgt")
    has_cp, has_cm = c < nc - 1, c > 0
    has_hp, has_hm = g < nh - 1, g > 0

    def lanes(k):
        return pl.ds(k * 128, 128)

    def loads(which):
        out = []
        for k in range(nk):
            if which < 3:
                out.append(pltpu.make_async_copy(
                    e_hbm.at[which, :, :, lanes(k)], e.at[which, pl.ds(0, sx), pl.ds(0, sz), k, :], load_sem.at[which]))
            elif which < 6:
                out.append(pltpu.make_async_copy(
                    h_hbm.at[which - 3, :, :, lanes(k)], h.at[which - 3, pl.ds(1, sx), pl.ds(1, sz), k, :], load_sem.at[which]))
            elif which == 6:
                out.append(pltpu.make_async_copy(t_hbm.at[:, :, lanes(k)], sigma.at[:, :, k, :], load_sem.at[which]))
            else:
                out.append(pltpu.make_async_copy(g_hbm.at[:, :, lanes(k)], tags.at[:, :, k, :], load_sem.at[which]))
        return out

    all_loads = [loads(w) for w in range(8)]
    for group in all_loads:
        for copy in group:
            copy.start()

    plan = [
        (has_cm, (c - 1, g), has_cp, e.at[pl.ds(1, 2), 0, pl.ds(0, sz)], xp),
        (has_hm, (c, g - 1), has_hp, e.at[pl.ds(0, 2), pl.ds(0, sx), 0], zp),
        (has_cp, (c + 1, g), has_cm, h.at[pl.ds(1, 2), sx, pl.ds(1, sz)], xm),
        (has_hp, (c, g + 1), has_hm, h.at[pl.ds(0, 2), pl.ds(1, sx), sz], zm),
        (has_cp & has_hm, (c + 1, g - 1), has_cm & has_hp, e.at[0, sx - 1, 0], cm),
        (has_cm & has_hp, (c - 1, g + 1), has_cp & has_hm, e.at[2, 0, sz - 1], cp),
    ]

    barrier = pltpu.get_barrier_semaphore()

    def greet(semaphore, device):
        pl.semaphore_signal(semaphore, inc=1, device_id=device, device_id_type=MESH)

    def along_col(semaphore):
        def one(i, _):
            greet(semaphore, (lax.rem(c + i, nc), g))
            return 0

        lax.fori_loop(1, nc, one, 0)

    def along_hgt(i, _):
        greet(barrier, (c, lax.rem(g + i, nh)))
        return 0

    lax.fori_loop(1, nh, along_hgt, 0)
    along_col(barrier)
    peers = nc + nh - 2
    for sends, device, _, _, _ in plan[4:]:
        @pl.when(sends)
        def _(device=device):
            greet(barrier, device)
        peers = peers + sends.astype(jnp.int32)
    zero_tile = jnp.zeros((8, 128), F32)
    for i in range(3):
        e[i, sx] = jnp.zeros((sz + 1, 8, 128), F32)
        h[i, 0] = jnp.zeros((sz + 1, 8, 128), F32)

    def clear(x, _):
        for i in range(3):
            e[i, x, sz] = zero_tile
            h[i, x + 1, 0] = zero_tile
        return 0

    lax.fori_loop(0, sx, clear, 0)
    pl.semaphore_wait(barrier, peers)
    along_col(ready)

    def copies(t):
        out = []
        for j, (sends, device, receives, src, buf) in enumerate(plan):
            out.append((sends, receives, pltpu.make_async_remote_copy(
                src_ref=src, dst_ref=buf.at[t], send_sem=ssem.at[t, j], recv_sem=rsem.at[t, j],
                device_id=device, device_id_type=MESH)))
        return out

    def update_h(x, nx, z0, nz):
        xs, xn, zs, zn, zw = pl.ds(x, nx), pl.ds(x + 1, nx), pl.ds(z0, nz), pl.ds(z0 + 1, nz), pl.ds(z0, nz + 1)
        ex, ey, ez = e[0, xs, zw], e[1, xs, zw], e[2, xs, zs]
        ey_x, ez_x = e[1, xn, zs], e[2, xn, zs]
        hx, hy, hz = h[0, xn, zn], h[1, xn, zn], h[2, xn, zn]
        ex, ex_z = ex[:, :nz], ex[:, 1:]
        ey, ey_z = ey[:, :nz], ey[:, 1:]
        hx = hx - COURANT * ((shifted_up(ez) - ez) - (ey_z - ey))
        hy = hy - COURANT * ((ex_z - ex) - (ez_x - ez))
        hz = hz - COURANT * ((ey_x - ey) - (shifted_up(ex) - ex))
        h[0, xn, zn] = hx
        h[1, xn, zn] = hy
        h[2, xn, zn] = hz

    def power_rows(x, z0, nz):
        return pl.ds(pl.multiple_of((x * sz + z0) * 8, 8), nz * 8)

    def update_e(x, nx, z0, nz):
        xs, xn, zs, zn, zw = pl.ds(x, nx), pl.ds(x + 1, nx), pl.ds(z0, nz), pl.ds(z0 + 1, nz), pl.ds(z0, nz + 1)
        hx, hy, hz = h[0, xn, zw], h[1, xn, zw], h[2, xn, zn]
        hy_x, hz_x = h[1, xs, zn], h[2, xs, zn]
        ex, ey, ez = e[0, xs, zs], e[1, xs, zs], e[2, xs, zs]
        a, b, s = ca[xs, zs], cb[xs, zs], sigma[xs, zs]
        lines = [power_rows(x + i, z0, nz) for i in range(nx)]
        p = [power[line].reshape(nz, 8, 128) for line in lines]
        hx_z, hx = hx[:, :nz], hx[:, 1:]
        hy_z, hy = hy[:, :nz], hy[:, 1:]
        ex = a * ex + b * ((hz - shifted_down(hz)) - (hy - hy_z))
        ey = a * ey + b * ((hx - hx_z) - (hz - hz_x))
        ez = a * ez + b * ((hy - hy_x) - (hx - shifted_down(hx)))
        e[0, xs, zs] = ex
        e[1, xs, zs] = ey
        e[2, xs, zs] = ez
        dissipated = s * (ex * ex + ey * ey + ez * ez)
        for i in range(nx):
            power[lines[i]] = (p[i] + dissipated[i]).reshape(nz * 8, 128)

    def over(x_lo, x_hi, nx, z_lo, z_hi, body):
        def at(i, _):
            body(x_lo + i * nx, nx, z_lo, z_hi - z_lo)
            return 0

        lax.fori_loop(0, (x_hi - x_lo) // nx, at, 0)

    def set_coefficients(x, nx, z0, nz):
        xs, zs = pl.ds(x, nx), pl.ds(z0, nz)
        s, a, b = coefficients(sigma[xs, zs], tags[xs, zs])
        sigma[xs, zs] = s
        ca[xs, zs] = a
        cb[xs, zs] = b
        for i in range(nx):
            power[power_rows(x + i, z0, nz)] = jnp.zeros((nz * 8, 128), F32)

    def corrections(t):
        @pl.when(has_cp)
        def _():
            h[1, sx, pl.ds(1, sz)] = h[1, sx, pl.ds(1, sz)] + COURANT * xp[t, 1]
            h[2, sx, pl.ds(1, sz)] = h[2, sx, pl.ds(1, sz)] - COURANT * xp[t, 0]

        @pl.when(has_cm)
        def _():
            h[1, 0, pl.ds(1, sz)] = xm[t, 0] + COURANT * e[2, 0, pl.ds(0, sz)]
            h[2, 0, pl.ds(1, sz)] = xm[t, 1] - COURANT * e[1, 0, pl.ds(0, sz)]

        @pl.when(has_cm & has_hp)
        def _():
            h[1, 0, sz] = h[1, 0, sz] - COURANT * cm[t]

        def rows(x, _):
            @pl.when(has_hp)
            def _():
                h[0, x + 1, sz] = h[0, x + 1, sz] + COURANT * zp[t, 1, x]
                h[1, x + 1, sz] = h[1, x + 1, sz] - COURANT * zp[t, 0, x]

            @pl.when(has_hm)
            def _():
                h[0, x + 1, 0] = zm[t, 0, x] + COURANT * e[1, x, 0]
                h[1, x + 1, 0] = zm[t, 1, x] - COURANT * e[0, x, 0]
            return 0

        lax.fori_loop(0, sx, rows, 0)

        @pl.when(has_cp & has_hm)
        def _():
            h[1, sx, 0] = h[1, sx, 0] + COURANT * cp[t]

    me = c * nh + g

    def partner(d):
        t = me ^ ((d * 11) % n_dev)
        return t, (t // nh, t % nh)

    def node_copy(d):
        t, device = partner(d)
        return pltpu.make_async_remote_copy(
            src_ref=nodes.at[t], dst_ref=recv_nodes.at[d], send_sem=node_out_sem, recv_sem=node_in_sem,
            device_id=device, device_id_type=MESH)

    def send_nodes(d, _):
        node_copy(d).start()
        return 0

    def block_copy(d):
        device = partner(d)[1]
        return pltpu.make_async_remote_copy(
            src_ref=send.at[d], dst_ref=recv.at[d], send_sem=out_sem,
            recv_sem=in_sem.at[d // GROUP], device_id=device, device_id_type=MESH)

    def gather(d):
        t = partner(d)[0]
        for r in range(cap):
            i = source[t, r]
            send[d, pl.ds(r, 1)] = power[pl.ds(i, 1)]

    for w in range(6):
        for copy in all_loads[w]:
            copy.wait()
    for t in range(STEPS):
        update_h(sx - 1, 1, 0, sz)
        update_h(0, sx - 1, sz - 1, 1)
        for sends, _, copy in copies(t):
            pl.when(sends)(copy.start)
        over(0, sx - 1, NXH, 0, sz - 1, update_h)
        if t == 0:
            for w in range(6, 8):
                for copy in all_loads[w]:
                    copy.wait()
            over(0, sx, 1, 0, sz, set_coefficients)
        over(1, sx - 1, NXE, 1, sz - 1, update_e)
        if t == 1:
            pl.semaphore_wait(ready, nc - 1)
            own_nodes = pltpu.make_async_copy(nodes.at[me], recv_nodes.at[0], local_sem.at[0])
            own_nodes.start()
            lax.fori_loop(1, n_dev, send_nodes, 0)
        for sends, receives, copy in copies(t):
            pl.when(sends)(copy.wait_send)
            pl.when(receives)(copy.wait_recv)
        corrections(t)
        update_e(0, 1, 0, sz)
        update_e(sx - 1, 1, 0, sz)
        update_e(1, sx - 2, 0, 1)
        update_e(1, sx - 2, sz - 1, 1)

    gather(0)
    gather(1)
    own = pltpu.make_async_copy(send.at[0], recv.at[0], local_sem.at[1])
    own.start()

    def exchange(d, _):
        gather(d)
        block_copy(d - 1).start()
        return 0

    lax.fori_loop(2, n_dev, exchange, 0)
    own.wait()
    own_nodes.wait()
    block_copy(n_dev - 1).start()
    others = pl.ds(0, n_dev - 1)
    pltpu.make_async_copy(recv_nodes.at[others], recv_nodes.at[others], node_in_sem).wait()
    pltpu.make_async_copy(recv_nodes.at[others], recv_nodes.at[others], node_out_sem).wait()

    n_nodes = enthalpy.shape[0]
    span = GROUP * cap
    count = lax.broadcasted_iota(jnp.int32, (n_nodes, span), 0).astype(F32) + 1.0

    def deposit(i, heat):
        tag = jnp.concatenate([recv_nodes[i * GROUP + j][:, :cap] for j in range(GROUP)], axis=1)
        pick = jnp.where(count == tag, 1.0, 0.0).astype(jnp.bfloat16)
        blocks = recv[pl.ds(i * GROUP, GROUP)].reshape(span, 128)
        high = blocks.astype(jnp.bfloat16)
        low = (blocks - high.astype(F32)).astype(jnp.bfloat16)
        both = jnp.dot(pick, jnp.concatenate([high, low], axis=1), preferred_element_type=F32)
        return heat + (both[:, :128] + both[:, 128:])

    def arrived(i, n):
        part = recv.at[pl.ds(0, n)]
        pltpu.make_async_copy(part, part, in_sem.at[i]).wait()

    def collect(i, heat):
        arrived(i, GROUP)
        return deposit(i, heat)

    arrived(0, GROUP - 1)
    heat = deposit(0, jnp.zeros((n_nodes, 128), F32))
    heat = lax.fori_loop(1, n_dev // GROUP, collect, heat)
    q = enthalpy[...] + (0.25 / STEPS) * heat
    out[...] = jnp.where(q < 0.0, q / 2.0, jnp.where(q > 1.0, (q - 1.0) / 3.0, 0.0))
    pltpu.make_async_copy(recv.at[others], recv.at[others], out_sem).wait()


def route_kernel(n_dev, cap, owner_ref, node_ref, source_ref, nodes_ref):
    rows = owner_ref.shape[0]
    who = lax.broadcasted_iota(jnp.int32, (n_dev, 128), 0)
    earlier = (lax.broadcasted_iota(jnp.int32, (128, 128), 0) < lax.broadcasted_iota(jnp.int32, (128, 128), 1)).astype(jnp.bfloat16)
    slot = lax.broadcasted_iota(jnp.int32, (128, 128), 0)
    lane = lax.broadcasted_iota(jnp.int32, (1, 128), 1).astype(F32)
    base = jnp.zeros((n_dev, 1), F32)
    sums = [jnp.zeros((n_dev, 128), F32) for _ in range(4)]
    for r in range(rows):
        own = owner_ref[pl.ds(r, 1), :]
        node = node_ref[pl.ds(r, 1), :] + 1
        hit = who == own
        hit_f = hit.astype(F32)
        hit_b = hit_f.astype(jnp.bfloat16)
        before = jnp.dot(hit_b, earlier, preferred_element_type=F32) + base
        rank = jnp.sum(hit_f * before, axis=0, keepdims=True).astype(jnp.int32)
        base = base + jnp.sum(hit_f, axis=1, keepdims=True)
        at = slot == rank
        values = (jnp.full((1, 128), float(r), F32), lane, (node // 16).astype(F32), (node % 16).astype(F32))
        for j, value in enumerate(values):
            sums[j] = sums[j] + lax.dot_general(
                hit_b, jnp.where(at, value, 0.0).astype(jnp.bfloat16), (((1,), (1,)), ((), ())), preferred_element_type=F32)
    source_ref[...] = (128.0 * sums[0] + sums[1]).astype(jnp.int32)
    nodes_ref[...] = (16.0 * sums[2] + sums[3]).reshape(nodes_ref.shape)


def store_kernel(e, h, e_hbm, h_hbm, sem):
    sx, sz = e_hbm.shape[1], e_hbm.shape[2]
    copies = []
    for i in range(3):
        for k in range(e_hbm.shape[3] // 128):
            copies.append(pltpu.make_async_copy(
                e.at[i, pl.ds(0, sx), pl.ds(0, sz), k, :], e_hbm.at[i, :, :, pl.ds(k * 128, 128)], sem))
            copies.append(pltpu.make_async_copy(
                h.at[i, pl.ds(1, sx), pl.ds(1, sz), k, :], h_hbm.at[i, :, :, pl.ds(k * 128, 128)], sem))
    for copy in copies:
        copy.start()
    for copy in copies:
        copy.wait()


def per_device(nc, nh, efield, hfield, cell_temp, region_tags, block_owner, block_node, node_enthalpy):
    sx, sz, sy = cell_temp.shape
    n_dev = nc * nh
    blocks = sx * sz * sy // 128
    cap = 2 * blocks // n_dev
    dma = pltpu.SemaphoreType.DMA

    def tiles(*shape):
        return pltpu.VMEM(shape + (8, 128), F32)

    def out(*shape):
        return jax.ShapeDtypeStruct(shape, F32)

    source, nodes = pl.pallas_call(
        lambda *refs: route_kernel(n_dev, cap, *refs),
        out_shape=(jax.ShapeDtypeStruct((n_dev, 128), jnp.int32), out(n_dev, 1, 128)),
        in_specs=[VMEM] * 2,
        out_specs=(VMEM, VMEM),
        name="route",
    )(block_owner.reshape(-1, 128), block_node.reshape(-1, 128))
    e, h, temp = pl.pallas_call(
        lambda *refs: fields_kernel(nc, nh, cap, *refs),
        out_shape=(tiles(3, sx + 1, sz + 1), tiles(3, sx + 1, sz + 1), out(*node_enthalpy.shape)),
        in_specs=[SMEM] + [HBM] * 4 + [VMEM, VMEM],
        out_specs=(VMEM, VMEM, VMEM),
        scratch_shapes=[
            pltpu.VMEM((sx * sz * 8, 128), F32), pltpu.VMEM((sx, sz, 8, 128), jnp.int32), tiles(sx, sz), tiles(sx, sz), tiles(sx, sz),
            tiles(STEPS, 2, sz), tiles(STEPS, 2, sx), tiles(STEPS, 2, sz), tiles(STEPS, 2, sx), tiles(STEPS), tiles(STEPS),
            pltpu.VMEM((n_dev, cap, 128), F32), pltpu.VMEM((n_dev, cap, 128), F32), pltpu.VMEM((n_dev, 1, 128), F32),
            dma((8,)), dma((STEPS, 6)), dma((STEPS, 6)), pltpu.SemaphoreType.REGULAR, dma((2,)), dma, dma((n_dev // GROUP,)), dma, dma,
        ],
        compiler_params=pltpu.CompilerParams(collective_id=0, has_side_effects=True, vmem_limit_bytes=48 << 20),
        name="fields",
    )(source, efield, hfield, cell_temp, region_tags, nodes, node_enthalpy)
    e_out, h_out = pl.pallas_call(
        store_kernel,
        out_shape=(out(3, sx, sz, sy), out(3, sx, sz, sy)),
        in_specs=[VMEM, VMEM],
        out_specs=(HBM, HBM),
        scratch_shapes=[dma],
        compiler_params=pltpu.CompilerParams(vmem_limit_bytes=24 << 20),
        name="store",
    )(e, h)
    return e_out, h_out, temp


def solution(mesh):
    placed = (
        P(None, "col", "hgt", None),
        P(None, "col", "hgt", None),
        P("col", "hgt", None),
        P("col", "hgt", None),
        P("col", "hgt", None, None, None, None),
        P("col", "hgt", None, None, None),
        P(("col", "hgt"), None),
    )
    nc, nh = mesh.shape["col"], mesh.shape["hgt"]
    return jax.shard_map(
        lambda *args: per_device(nc, nh, *args),
        mesh=mesh,
        in_specs=placed,
        out_specs=(P(None, "col", "hgt", None), P(None, "col", "hgt", None), P(("col", "hgt"), None)),
        check_vma=False,
    )
```

time: 104 us -> 94.9 us (0.913)
  Pallas kernels: 99.2 us -> 89.9 us
    pallas_call x3 -> x2, Pallas kernels: 92.9 us -> 82.6 us  [the longest x1 79.1 us: per_device(): pl.pallas_call(lambda *refs: fields_kernel(nc, nh, cap, *refs), out_shape...]
    unnamed x9 -> x5, local copies, waits for them, and re-layouts: 2.58 us -> 2.57 us
where the time goes in v3:
time: 94.9 us; the launch traced here: 94.6 us
  Pallas kernels  89.9 us (95%)
  local copies, waits for them, and re-layouts  4.04 us (4%)
    pallas_call x1, Pallas kernels, per_device(): pl.pallas_call(lambda *refs: fields_kernel(nc, nh, cap, *refs), out_shape...  79.1 us
    pallas_call x1, Pallas kernels, per_device(): pl.pallas_call(lambda *refs: route_kernel(n_dev, cap, *refs), out_shape=(...  7.27 us
    pallas_call x1, Pallas kernels, per_device(): pl.pallas_call(store_kernel, out_shape=(out(3, sx, sz, sy), out(3, sx, sz...  3.58 us
    unnamed x5, local copies, waits for them, and re-layouts  2.57 us

profile of v3, /device:TPU:1, one launch (start us, length us, event | category | flops | bytes accessed | tf_op | source)
XLA Modules:
  0.0 94.6 jit_solution(4158873655841912773)
XLA Ops:
  0.6 0.9 copy.12
  1.6 0.7 reshape.12.refs_0_
  2.3 0.9 copy.13
  3.3 0.7 reshape.13.refs_1_
  4.0 7.3 %route.1 = (s32[128,128]{1,0:T(8,128)}, f32[128,1,128]{2,1,0:T(1,128)}) custom-call(s32[24,128]{1,0:T(8,128)} %reshape.12.refs_0_, s32[24,128]{1,0:T(8,128)} %reshape.13.refs_1_), custom_call_target="tpu_custom_call" | custom-call | tf_op jit(solution)/shard_map/route/pallas_call | solution.py:387
  11.3 79.1 %fields.1 = (f32[3,17,25,8,128]{4,3,2,1,0:T(8,128)S(1)}, f32[3,17,25,8,128]{4,3,2,1,0:T(8,128)S(1)}, f32[384,128]{1,0:T(8,128)}) custom-call(s32[128,128]{1,0:T(8,128)} %get-tuple-element.10.refs_0_, f32[3,16,24,1024]{3,2,1,0:T(8,128)} %refs_1_.1, f32[3,16,24,1024]{3,2,1,0:T(8,128)} %refs_2_.1, f32[16,24,1024]{2,1,0:T(8,128)} %refs_3_.1, ...), custom_call_target="tpu_custom_call" | custom-call | tf_op jit(solution)/shard_map/fields/pallas_call | solution.py:394
  90.3 0.0 copy-start
  90.4 3.6 %store.1 = (f32[3,16,24,1024]{3,2,1,0:T(8,128)}, f32[3,16,24,1024]{3,2,1,0:T(8,128)}) custom-call(f32[3,17,25,8,128]{4,3,2,1,0:T(8,128)S(1)} %get-tuple-element.12.e, f32[3,17,25,8,128]{4,3,2,1,0:T(8,128)S(1)} %get-tuple-element.13.h), custom_call_target="tpu_custom_call" | custom-call | tf_op jit(solution)/shard_map/store/pallas_call | solution.py:408
  93.9 0.0 copy-done
  94.0 0.7 copy.15
Async XLA Ops:
  90.3 3.6 %copy-start = (f32[384,128]{1,0:T(8,128)S(1)}, f32[384,128]{1,0:T(8,128)}, u32[]{:S(2)}) copy-start(f32[384,128]{1,0:T(8,128)} %get-tuple-element.22) | copy-start | bytes 589828

commit v4 on v3

--- a/solution.py
+++ b/solution.py
@@ -14,7 +14,6 @@
 F32 = jnp.float32
 HBM = pl.BlockSpec(memory_space=pltpu.HBM)
 VMEM = pl.BlockSpec(memory_space=pltpu.VMEM)
-SMEM = pl.BlockSpec(memory_space=pltpu.SMEM)
 
 
 def shifted_up(f):
@@ -50,8 +49,41 @@
     return sigma, (eps2 - half) * inv, (2.0 * COURANT) * inv
 
 
-def fields_kernel(nc, nh, cap, source, e_hbm, h_hbm, t_hbm, g_hbm, nodes, enthalpy, e, h, out,
-                  power, tags, sigma, ca, cb, xp, zp, xm, zm, cm, cp, send, recv, recv_nodes,
+def route(n_dev, cap, owner_ref, node_ref, source_ref, nodes_ref):
+    sx, nk, sz = owner_ref.shape
+    per = max(p for p in range(1, 128 // sz + 1) if sx % p == 0)
+    who = lax.broadcasted_iota(jnp.int32, (n_dev, 128), 0)
+    earlier = (lax.broadcasted_iota(jnp.int32, (128, 128), 0) < lax.broadcasted_iota(jnp.int32, (128, 128), 1)).astype(jnp.bfloat16)
+    slot = lax.broadcasted_iota(jnp.int32, (cap, 128), 0)
+    lane = lax.broadcasted_iota(jnp.int32, (1, 128), 1).astype(F32)
+    first = lax.broadcasted_iota(jnp.int32, (1, 4 * cap), 1) < cap
+    base = jnp.zeros((n_dev, 1), F32)
+    sums = jnp.zeros((n_dev, 4 * cap), F32)
+    for q in range(sx // per):
+        fill = jnp.full((nk, 128 - per * sz), -1, jnp.int32)
+        owners = jnp.concatenate([owner_ref[q * per + i] for i in range(per)] + [fill], axis=1)
+        tags = jnp.concatenate([node_ref[q * per + i] for i in range(per)] + [fill], axis=1) + 1
+        tags_hi = (tags // 16).astype(F32)
+        tags_lo = (tags % 16).astype(F32)
+        for k in range(nk):
+            hit = who == owners[k : k + 1]
+            hit_f = hit.astype(F32)
+            hit_b = hit_f.astype(jnp.bfloat16)
+            before = jnp.dot(hit_b, earlier, preferred_element_type=F32) + base
+            rank = jnp.sum(hit_f * before, axis=0, keepdims=True).astype(jnp.int32)
+            base = base + jnp.sum(hit_f, axis=1, keepdims=True)
+            at = slot == rank
+            values = (1.0, lane, tags_hi[k : k + 1], tags_lo[k : k + 1])
+            table = jnp.concatenate([jnp.where(at, value, 0.0) for value in values], axis=0).astype(jnp.bfloat16)
+            got = lax.dot_general(hit_b, table, (((1,), (1,)), ((), ())), preferred_element_type=F32)
+            sums = sums + got * jnp.where(first, float(q * per * sz * nk + k), 1.0)
+    source_ref[:, :cap] = (sums[:, :cap] + float(nk) * sums[:, cap : 2 * cap]).astype(jnp.int32)
+    tag = 16.0 * sums[:, 2 * cap : 3 * cap] + sums[:, 3 * cap :]
+    nodes_ref[...] = jnp.concatenate([tag, jnp.zeros((n_dev, 128 - cap), F32)], axis=1).reshape(n_dev, 1, 128)
+
+
+def fields_kernel(nc, nh, cap, e_hbm, h_hbm, t_hbm, g_hbm, owner, node, e, h, heat_out,
+                  source_vmem, source, nodes, power, tags, sigma, ca, cb, xp, zp, xm, zm, cm, cp, send, recv, recv_nodes,
                   load_sem, ssem, rsem, ready, local_sem, out_sem, in_sem, node_out_sem, node_in_sem):
     n_dev = nc * nh
     sx, sz = t_hbm.shape[0], t_hbm.shape[1]
@@ -80,8 +112,8 @@
         return out
 
     all_loads = [loads(w) for w in range(8)]
-    for group in all_loads:
-        for copy in group:
+    for w in (6, 7, 0, 1, 2, 3, 4, 5):
+        for copy in all_loads[w]:
             copy.start()
 
     plan = [
@@ -129,9 +161,6 @@
         return 0
 
     lax.fori_loop(0, sx, clear, 0)
-    pl.semaphore_wait(barrier, peers)
-    along_col(ready)
-
     def copies(t):
         out = []
         for j, (sends, device, receives, src, buf) in enumerate(plan):
@@ -251,9 +280,19 @@
     def gather(d):
         t = partner(d)[0]
         for r in range(cap):
-            i = source[t, r]
+            i = jnp.clip(source[t, r], 0, sx * sz * 8 - 1)
             send[d, pl.ds(r, 1)] = power[pl.ds(i, 1)]
 
+    route(n_dev, cap, owner, node, source_vmem, nodes)
+    for w in range(6, 8):
+        for copy in all_loads[w]:
+            copy.wait()
+    over(0, sx, 1, 0, sz, set_coefficients)
+    to_smem = pltpu.make_async_copy(source_vmem, source, local_sem.at[2])
+    to_smem.start()
+    to_smem.wait()
+    pl.semaphore_wait(barrier, peers)
+    along_col(ready)
     for w in range(6):
         for copy in all_loads[w]:
             copy.wait()
@@ -263,11 +302,6 @@
         for sends, _, copy in copies(t):
             pl.when(sends)(copy.start)
         over(0, sx - 1, NXH, 0, sz - 1, update_h)
-        if t == 0:
-            for w in range(6, 8):
-                for copy in all_loads[w]:
-                    copy.wait()
-            over(0, sx, 1, 0, sz, set_coefficients)
         over(1, sx - 1, NXE, 1, sz - 1, update_e)
         if t == 1:
             pl.semaphore_wait(ready, nc - 1)
@@ -301,7 +335,7 @@
     pltpu.make_async_copy(recv_nodes.at[others], recv_nodes.at[others], node_in_sem).wait()
     pltpu.make_async_copy(recv_nodes.at[others], recv_nodes.at[others], node_out_sem).wait()
 
-    n_nodes = enthalpy.shape[0]
+    n_nodes = heat_out.shape[0]
     span = GROUP * cap
     count = lax.broadcasted_iota(jnp.int32, (n_nodes, span), 0).astype(F32) + 1.0
 
@@ -325,38 +359,11 @@
     arrived(0, GROUP - 1)
     heat = deposit(0, jnp.zeros((n_nodes, 128), F32))
     heat = lax.fori_loop(1, n_dev // GROUP, collect, heat)
-    q = enthalpy[...] + (0.25 / STEPS) * heat
-    out[...] = jnp.where(q < 0.0, q / 2.0, jnp.where(q > 1.0, (q - 1.0) / 3.0, 0.0))
+    heat_out[...] = heat
     pltpu.make_async_copy(recv.at[others], recv.at[others], out_sem).wait()
 
 
-def route_kernel(n_dev, cap, owner_ref, node_ref, source_ref, nodes_ref):
-    rows = owner_ref.shape[0]
-    who = lax.broadcasted_iota(jnp.int32, (n_dev, 128), 0)
-    earlier = (lax.broadcasted_iota(jnp.int32, (128, 128), 0) < lax.broadcasted_iota(jnp.int32, (128, 128), 1)).astype(jnp.bfloat16)
-    slot = lax.broadcasted_iota(jnp.int32, (128, 128), 0)
-    lane = lax.broadcasted_iota(jnp.int32, (1, 128), 1).astype(F32)
-    base = jnp.zeros((n_dev, 1), F32)
-    sums = [jnp.zeros((n_dev, 128), F32) for _ in range(4)]
-    for r in range(rows):
-        own = owner_ref[pl.ds(r, 1), :]
-        node = node_ref[pl.ds(r, 1), :] + 1
-        hit = who == own
-        hit_f = hit.astype(F32)
-        hit_b = hit_f.astype(jnp.bfloat16)
-        before = jnp.dot(hit_b, earlier, preferred_element_type=F32) + base
-        rank = jnp.sum(hit_f * before, axis=0, keepdims=True).astype(jnp.int32)
-        base = base + jnp.sum(hit_f, axis=1, keepdims=True)
-        at = slot == rank
-        values = (jnp.full((1, 128), float(r), F32), lane, (node // 16).astype(F32), (node % 16).astype(F32))
-        for j, value in enumerate(values):
-            sums[j] = sums[j] + lax.dot_general(
-                hit_b, jnp.where(at, value, 0.0).astype(jnp.bfloat16), (((1,), (1,)), ((), ())), preferred_element_type=F32)
-    source_ref[...] = (128.0 * sums[0] + sums[1]).astype(jnp.int32)
-    nodes_ref[...] = (16.0 * sums[2] + sums[3]).reshape(nodes_ref.shape)
-
-
-def store_kernel(e, h, e_hbm, h_hbm, sem):
+def store_kernel(e, h, heat, enthalpy, e_hbm, h_hbm, temp, sem):
     sx, sz = e_hbm.shape[1], e_hbm.shape[2]
     copies = []
     for i in range(3):
@@ -367,6 +374,8 @@
                 h.at[i, pl.ds(1, sx), pl.ds(1, sz), k, :], h_hbm.at[i, :, :, pl.ds(k * 128, 128)], sem))
     for copy in copies:
         copy.start()
+    q = enthalpy[...] + (0.25 / STEPS) * heat[...]
+    temp[...] = jnp.where(q < 0.0, q / 2.0, jnp.where(q > 1.0, (q - 1.0) / 3.0, 0.0))
     for copy in copies:
         copy.wait()
 
@@ -384,37 +393,33 @@
     def out(*shape):
         return jax.ShapeDtypeStruct(shape, F32)
 
-    source, nodes = pl.pallas_call(
-        lambda *refs: route_kernel(n_dev, cap, *refs),
-        out_shape=(jax.ShapeDtypeStruct((n_dev, 128), jnp.int32), out(n_dev, 1, 128)),
-        in_specs=[VMEM] * 2,
-        out_specs=(VMEM, VMEM),
-        name="route",
-    )(block_owner.reshape(-1, 128), block_node.reshape(-1, 128))
-    e, h, temp = pl.pallas_call(
+    def native(table):
+        return table.reshape(sx, sz, sy // 128).transpose(0, 2, 1)
+
+    e, h, heat = pl.pallas_call(
         lambda *refs: fields_kernel(nc, nh, cap, *refs),
-        out_shape=(tiles(3, sx + 1, sz + 1), tiles(3, sx + 1, sz + 1), out(*node_enthalpy.shape)),
-        in_specs=[SMEM] + [HBM] * 4 + [VMEM, VMEM],
+        out_shape=(tiles(3, sx + 1, sz + 1), tiles(3, sx + 1, sz + 1), pltpu.VMEM(node_enthalpy.shape, F32)),
+        in_specs=[HBM] * 4 + [VMEM, VMEM],
         out_specs=(VMEM, VMEM, VMEM),
         scratch_shapes=[
+            pltpu.VMEM((n_dev, 128), jnp.int32), pltpu.SMEM((n_dev, 128), jnp.int32), pltpu.VMEM((n_dev, 1, 128), F32),
             pltpu.VMEM((sx * sz * 8, 128), F32), pltpu.VMEM((sx, sz, 8, 128), jnp.int32), tiles(sx, sz), tiles(sx, sz), tiles(sx, sz),
             tiles(STEPS, 2, sz), tiles(STEPS, 2, sx), tiles(STEPS, 2, sz), tiles(STEPS, 2, sx), tiles(STEPS), tiles(STEPS),
             pltpu.VMEM((n_dev, cap, 128), F32), pltpu.VMEM((n_dev, cap, 128), F32), pltpu.VMEM((n_dev, 1, 128), F32),
-            dma((8,)), dma((STEPS, 6)), dma((STEPS, 6)), pltpu.SemaphoreType.REGULAR, dma((2,)), dma, dma((n_dev // GROUP,)), dma, dma,
+            dma((8,)), dma((STEPS, 6)), dma((STEPS, 6)), pltpu.SemaphoreType.REGULAR, dma((3,)), dma, dma((n_dev // GROUP,)), dma, dma,
         ],
         compiler_params=pltpu.CompilerParams(collective_id=0, has_side_effects=True, vmem_limit_bytes=48 << 20),
         name="fields",
-    )(source, efield, hfield, cell_temp, region_tags, nodes, node_enthalpy)
-    e_out, h_out = pl.pallas_call(
+    )(efield, hfield, cell_temp, region_tags, native(block_owner), native(block_node))
+    return pl.pallas_call(
         store_kernel,
-        out_shape=(out(3, sx, sz, sy), out(3, sx, sz, sy)),
-        in_specs=[VMEM, VMEM],
-        out_specs=(HBM, HBM),
+        out_shape=(out(3, sx, sz, sy), out(3, sx, sz, sy), out(*node_enthalpy.shape)),
+        in_specs=[VMEM] * 4,
+        out_specs=(HBM, HBM, VMEM),
         scratch_shapes=[dma],
         compiler_params=pltpu.CompilerParams(vmem_limit_bytes=24 << 20),
         name="store",
-    )(e, h)
-    return e_out, h_out, temp
+    )(e, h, heat, node_enthalpy)
 
 
 def solution(mesh):

time: 94.9 us -> 86.1 us (0.907)
  Pallas kernels: 89.9 us -> 85.2 us
  local copies, waits for them, and re-layouts: 4.04 us -> 0.01 us
    pallas_call x1 -> x0, Pallas kernels: 7.27 us -> none  [per_device(): pl.pallas_call(lambda *refs: route_kernel(n_dev, cap, *refs), out_shape=(...]
    unnamed x5 -> x2, local copies, waits for them, and re-layouts: 2.57 us -> 0.01 us
    pallas_call x1, Pallas kernels: 79.1 us -> 81 us  [per_device(): pl.pallas_call(lambda *refs: fields_kernel(nc, nh, cap, *refs), out_shape...]
    reshape x2 -> x0, local copies, waits for them, and re-layouts: 1.47 us -> none  [the longest x1 0.73 us: per_device(): block_owner.reshape(-1, 128)]
where the time goes in v4:
time: 86.1 us; the launch traced here: 85.9 us
  Pallas kernels  85.2 us (99%)
    pallas_call x1, Pallas kernels, per_device(): pl.pallas_call(lambda *refs: fields_kernel(nc, nh, cap, *refs), out_shape...  81 us
    pallas_call x1, Pallas kernels, per_device(): pl.pallas_call(store_kernel, out_shape=(out(3, sx, sz, sy), out(3, sx, sz...  4.25 us

profile of v4, /device:TPU:1, one launch (start us, length us, event | category | flops | bytes accessed | tf_op | source)
XLA Modules:
  0.0 85.9 jit_solution(8714913823583462592)
XLA Ops:
  0.6 0.0 copy-start
  0.6 81.0 %fields.1 = (f32[3,17,25,8,128]{4,3,2,1,0:T(8,128)S(1)}, f32[3,17,25,8,128]{4,3,2,1,0:T(8,128)S(1)}, f32[384,128]{1,0:T(8,128)S(1)}) custom-call(f32[3,16,24,1024]{3,2,1,0:T(8,128)} %refs_0_.1, f32[3,16,24,1024]{3,2,1,0:T(8,128)} %refs_1_.1, f32[16,24,1024]{2,1,0:T(8,128)} %refs_2_.1, s32[16,24,1024]{2,1,0:T(8,128)} %refs_3_.1, s32[16,8,24]{2,1,0:T(8,128)} %bitcast.6, ...), custom_call_target="tpu_custom_call" | custom-call | tf_op jit(solution)/shard_map/fields/pallas_call | solution.py:399
  81.6 0.0 copy-done
  81.6 4.3 %store.1 = (f32[3,16,24,1024]{3,2,1,0:T(8,128)}, f32[3,16,24,1024]{3,2,1,0:T(8,128)}, f32[384,128]{1,0:T(8,128)}) custom-call(f32[3,17,25,8,128]{4,3,2,1,0:T(8,128)S(1)} %get-tuple-element.6.e, f32[3,17,25,8,128]{4,3,2,1,0:T(8,128)S(1)} %get-tuple-element.7.h, f32[384,128]{1,0:T(8,128)S(1)} %get-tuple-element.8.heat, f32[384,128]{1,0:T(8,128)S(1)} %copy-done), custom_call_target="tpu_custom_call" | custom-call | tf_op jit(solution)/shard_map/store/pallas_call | solution.py:414
Async XLA Ops:
  0.6 81.0 %copy-start = (f32[384,128]{1,0:T(8,128)S(1)}, f32[384,128]{1,0:T(8,128)}, u32[]{:S(2)}) copy-start(f32[384,128]{1,0:T(8,128)} %enthalpy.1) | copy-start | bytes 589828

commit v5 on v4

--- a/solution.py
+++ b/solution.py
@@ -7,8 +7,6 @@
 
 STEPS = 4
 COURANT = 0.55
-NXH = 1
-NXE = 1
 GROUP = 8
 MESH = pl.DeviceIdType.MESH
 F32 = jnp.float32
@@ -90,6 +88,7 @@
     nk = t_hbm.shape[2] // 128
     c = lax.axis_index("col")
     g = lax.axis_index("hgt")
+    planes_h = max(p for p in (1, 2, 3) if (sx - 1) % p == 0)
     has_cp, has_cm = c < nc - 1, c > 0
     has_hp, has_hm = g < nh - 1, g > 0
 
@@ -206,6 +205,10 @@
         for i in range(nx):
             power[lines[i]] = (p[i] + dissipated[i]).reshape(nz * 8, 128)
 
+    def update_e_in_halves(x, nx, z0, nz):
+        update_e(x, nx, z0, nz // 2)
+        update_e(x, nx, z0 + nz // 2, nz - nz // 2)
+
     def over(x_lo, x_hi, nx, z_lo, z_hi, body):
         def at(i, _):
             body(x_lo + i * nx, nx, z_lo, z_hi - z_lo)
@@ -237,19 +240,17 @@
         def _():
             h[1, 0, sz] = h[1, 0, sz] - COURANT * cm[t]
 
-        def rows(x, _):
-            @pl.when(has_hp)
-            def _():
-                h[0, x + 1, sz] = h[0, x + 1, sz] + COURANT * zp[t, 1, x]
-                h[1, x + 1, sz] = h[1, x + 1, sz] - COURANT * zp[t, 0, x]
-
-            @pl.when(has_hm)
-            def _():
-                h[0, x + 1, 0] = zm[t, 0, x] + COURANT * e[1, x, 0]
-                h[1, x + 1, 0] = zm[t, 1, x] - COURANT * e[0, x, 0]
-            return 0
-
-        lax.fori_loop(0, sx, rows, 0)
+        planes, own = pl.ds(1, sx), pl.ds(0, sx)
+
+        @pl.when(has_hp)
+        def _():
+            h[0, planes, sz] = h[0, planes, sz] + COURANT * zp[t, 1]
+            h[1, planes, sz] = h[1, planes, sz] - COURANT * zp[t, 0]
+
+        @pl.when(has_hm)
+        def _():
+            h[0, planes, 0] = zm[t, 0] + COURANT * e[1, own, 0]
+            h[1, planes, 0] = zm[t, 1] - COURANT * e[0, own, 0]
 
         @pl.when(has_cp & has_hm)
         def _():
@@ -301,8 +302,8 @@
         update_h(0, sx - 1, sz - 1, 1)
         for sends, _, copy in copies(t):
             pl.when(sends)(copy.start)
-        over(0, sx - 1, NXH, 0, sz - 1, update_h)
-        over(1, sx - 1, NXE, 1, sz - 1, update_e)
+        over(0, sx - 1, planes_h, 0, sz - 1, update_h)
+        over(1, sx - 1, 1, 1, sz - 1, update_e_in_halves)
         if t == 1:
             pl.semaphore_wait(ready, nc - 1)
             own_nodes = pltpu.make_async_copy(nodes.at[me], recv_nodes.at[0], local_sem.at[0])

time: 86.1 us -> 84.7 us (0.984)
  Pallas kernels: 85.2 us -> 83.9 us
    pallas_call x1, Pallas kernels: 81 us -> 79.6 us  [per_device(): pl.pallas_call(lambda *refs: fields_kernel(nc, nh, cap, *refs), out_shape...]
where the time goes in v5:
time: 84.7 us; the launch traced here: 84.5 us
  Pallas kernels  83.9 us (99%)
    pallas_call x1, Pallas kernels, per_device(): pl.pallas_call(lambda *refs: fields_kernel(nc, nh, cap, *refs), out_shape...  79.6 us
    pallas_call x1, Pallas kernels, per_device(): pl.pallas_call(store_kernel, out_shape=(out(3, sx, sz, sy), out(3, sx, sz...  4.25 us

profile of v5, /device:TPU:1, one launch (start us, length us, event | category | flops | bytes accessed | tf_op | source)
XLA Modules:
  0.0 84.5 jit_solution(564604782384554887)
XLA Ops:
  0.6 0.0 copy-start
  0.6 79.6 %fields.1 = (f32[3,17,25,8,128]{4,3,2,1,0:T(8,128)S(1)}, f32[3,17,25,8,128]{4,3,2,1,0:T(8,128)S(1)}, f32[384,128]{1,0:T(8,128)S(1)}) custom-call(f32[3,16,24,1024]{3,2,1,0:T(8,128)} %refs_0_.1, f32[3,16,24,1024]{3,2,1,0:T(8,128)} %refs_1_.1, f32[16,24,1024]{2,1,0:T(8,128)} %refs_2_.1, s32[16,24,1024]{2,1,0:T(8,128)} %refs_3_.1, s32[16,8,24]{2,1,0:T(8,128)} %bitcast.6, ...), custom_call_target="tpu_custom_call" | custom-call | tf_op jit(solution)/shard_map/fields/pallas_call | solution.py:400
  80.2 0.0 copy-done
  80.3 4.3 %store.1 = (f32[3,16,24,1024]{3,2,1,0:T(8,128)}, f32[3,16,24,1024]{3,2,1,0:T(8,128)}, f32[384,128]{1,0:T(8,128)}) custom-call(f32[3,17,25,8,128]{4,3,2,1,0:T(8,128)S(1)} %get-tuple-element.6.e, f32[3,17,25,8,128]{4,3,2,1,0:T(8,128)S(1)} %get-tuple-element.7.h, f32[384,128]{1,0:T(8,128)S(1)} %get-tuple-element.8.heat, f32[384,128]{1,0:T(8,128)S(1)} %copy-done), custom_call_target="tpu_custom_call" | custom-call | tf_op jit(solution)/shard_map/store/pallas_call | solution.py:415
Async XLA Ops:
  0.6 79.6 %copy-start = (f32[384,128]{1,0:T(8,128)S(1)}, f32[384,128]{1,0:T(8,128)}, u32[]{:S(2)}) copy-start(f32[384,128]{1,0:T(8,128)} %enthalpy.1) | copy-start | bytes 589828

commit v6 on v5

--- a/solution.py
+++ b/solution.py
@@ -294,14 +294,24 @@
     to_smem.wait()
     pl.semaphore_wait(barrier, peers)
     along_col(ready)
-    for w in range(6):
+    def start(t, which):
+        group = copies(t)
+        for j in which:
+            pl.when(group[j][0])(group[j][2].start)
+
+    for w in range(3):
+        for copy in all_loads[w]:
+            copy.wait()
+    start(0, (0, 1))
+    for w in range(3, 6):
         for copy in all_loads[w]:
             copy.wait()
     for t in range(STEPS):
         update_h(sx - 1, 1, 0, sz)
+        if t > 0:
+            start(t, (0, 1))
         update_h(0, sx - 1, sz - 1, 1)
-        for sends, _, copy in copies(t):
-            pl.when(sends)(copy.start)
+        start(t, (4, 5, 2, 3))
         over(0, sx - 1, planes_h, 0, sz - 1, update_h)
         over(1, sx - 1, 1, 1, sz - 1, update_e_in_halves)
         if t == 1:

time: 84.7 us -> 84.2 us (level)
  no operation moved by 1% of the time
where the time goes in v6:
time: 84.2 us; the launch traced here: 84 us
  Pallas kernels  83.4 us (99%)
    pallas_call x1, Pallas kernels, per_device(): pl.pallas_call(lambda *refs: fields_kernel(nc, nh, cap, *refs), out_shape...  79.1 us
    pallas_call x1, Pallas kernels, per_device(): pl.pallas_call(store_kernel, out_shape=(out(3, sx, sz, sy), out(3, sx, sz...  4.25 us

profile of v6, /device:TPU:1, one launch (start us, length us, event | category | flops | bytes accessed | tf_op | source)
XLA Modules:
  0.0 84.0 jit_solution(836146247992469140)
XLA Ops:
  0.6 0.0 copy-start
  0.6 79.1 %fields.1 = (f32[3,17,25,8,128]{4,3,2,1,0:T(8,128)S(1)}, f32[3,17,25,8,128]{4,3,2,1,0:T(8,128)S(1)}, f32[384,128]{1,0:T(8,128)S(1)}) custom-call(f32[3,16,24,1024]{3,2,1,0:T(8,128)} %refs_0_.1, f32[3,16,24,1024]{3,2,1,0:T(8,128)} %refs_1_.1, f32[16,24,1024]{2,1,0:T(8,128)} %refs_2_.1, s32[16,24,1024]{2,1,0:T(8,128)} %refs_3_.1, s32[16,8,24]{2,1,0:T(8,128)} %bitcast.6, ...), custom_call_target="tpu_custom_call" | custom-call | tf_op jit(solution)/shard_map/fields/pallas_call | solution.py:410
  79.7 0.0 copy-done
  79.8 4.3 %store.1 = (f32[3,16,24,1024]{3,2,1,0:T(8,128)}, f32[3,16,24,1024]{3,2,1,0:T(8,128)}, f32[384,128]{1,0:T(8,128)}) custom-call(f32[3,17,25,8,128]{4,3,2,1,0:T(8,128)S(1)} %get-tuple-element.6.e, f32[3,17,25,8,128]{4,3,2,1,0:T(8,128)S(1)} %get-tuple-element.7.h, f32[384,128]{1,0:T(8,128)S(1)} %get-tuple-element.8.heat, f32[384,128]{1,0:T(8,128)S(1)} %copy-done), custom_call_target="tpu_custom_call" | custom-call | tf_op jit(solution)/shard_map/store/pallas_call | solution.py:425
Async XLA Ops:
  0.6 79.1 %copy-start = (f32[384,128]{1,0:T(8,128)S(1)}, f32[384,128]{1,0:T(8,128)}, u32[]{:S(2)}) copy-start(f32[384,128]{1,0:T(8,128)} %enthalpy.1) | copy-start | bytes 589828
